TPU v7x, 256 devices: a whole 4x4x8 slice. The times are simulated.
256 devices in a mesh: gx: 4 (over x), vert: 64 (over y, z, core).
Axes of the slice: x: 4, y: 4, z: 8, core: 2. Of those that a mesh axis runs over, the one named last changes fastest.
Arguments:
- dist: float32 [2, 4096, 24576], P(None, 'vert', 'gx'), may hold values from -6 to 6
- factors: float32 [2, 4096, 128], P(None, 'vert', 'gx'), may hold values from 0.95 to 0.999
- velocity: float32 [3, 2, 4096], P(None, None, 'vert'), may hold values from -3 to 3
- weights: float32 [13, 2, 4096], P(None, None, 'vert'), may hold values from -0.0625 to 0.0625
- relax: float32 [2, 4096], P(None, 'vert'), may hold values from 0.1 to 0.9
Outputs:
- updated: float32 [2, 4096, 24576], P(None, 'vert', 'gx')
- macro: float32 [13, 24576], P(None, 'gx')
All inputs are finite; a program needn't handle non-finite values.
Results may differ from a plain program's by a relative error of at most 0.000071.
Values sent between devices are 32-bit elements; how exact they have to be, the bound alone decides.
A program may use at most 64 MiB of HBM per device.

v0:
```python
import jax
import jax.numpy as jnp
from jax import lax
from jax.sharding import PartitionSpec as P

SMOOTH = 4


smooth_rate = 0.24


def padded_2(cells, sides, width):
    for axis, dim in sides:
        count = lax.axis_size(axis)
        ends = count - 1
        head = lax.slice_in_dim(cells, 0, width, axis=dim)
        tail = lax.slice_in_dim(cells, cells.shape[dim] - width, cells.shape[dim], axis=dim)
        cells = jnp.concatenate(
            [
                lax.ppermute(tail, axis, [(i, (i + 1) % count) for i in range(ends)]),
                cells,
                lax.ppermute(head, axis, [((i + 1) % count, i) for i in range(ends)]),
            ],
            axis=dim,
        )
    return cells


def shifted(value, axis, steps):
    count = lax.axis_size(axis)
    leading, last = (max(0, -steps), min(count, count - steps))
    return lax.ppermute(value, axis, [(source, source + steps) for source in range(leading, last)])


def equilibrium(moments, speed_x, speed_y, speed_z):
    density = 1.0 + 0.5 * jnp.tanh(moments[0])
    flow_x = 0.5 * jnp.tanh(moments[1])
    flow_y = 0.5 * jnp.tanh(moments[2])
    flow_z = 0.5 * jnp.tanh(moments[3])
    temper = 1.0 + 0.5 * jnp.tanh(moments[4])
    stress = 0.2 * jnp.tanh(moments[5:10])
    fluxes = 0.2 * jnp.tanh(moments[10:13])
    rel_x = speed_x - flow_x
    rel_y = speed_y - flow_y
    rel_z = speed_z - flow_z
    square = rel_x * rel_x + rel_y * rel_y + rel_z * rel_z
    inverse = 1.0 / temper
    shape_term = (
        stress[0] * rel_x * rel_y
        + stress[1] * rel_x * rel_z
        + stress[2] * rel_y * rel_z
        + 0.5 * stress[3] * (rel_x * rel_x - rel_z * rel_z)
        + 0.5 * stress[4] * (rel_y * rel_y - rel_z * rel_z)
    )
    heat_term = (fluxes[0] * rel_x + fluxes[1] * rel_y + fluxes[2] * rel_z) * (
        0.5 * square * inverse - 2.5
    )
    return (
        density
        * inverse
        * jnp.sqrt(inverse)
        * jnp.exp(-0.5 * square * inverse)
        * (1.0 + (shape_term + heat_term) * inverse)
    )


def smooth_step(moments, padded):
    coef = 1.0 / (1.0 + moments[0] * moments[0])
    return moments + smooth_rate * coef * (padded[:, 2:] - 2.0 * moments + padded[:, :-2])


def smooth_whole(moments):
    for step in range(SMOOTH):
        padded = padded_2(moments, (("gx", 1),), 1)
        moments = smooth_step(moments, padded)
    return moments


def per_device(dist, factors, velocity, weights, relax):
    cells = factors.shape[2]
    vel_dev = dist.shape[1]
    plane = dist.shape[2] // cells
    grid = dist.reshape(2, vel_dev, cells, plane)
    source = jnp.sqrt(1.0 - factors * factors)[..., None] * grid
    logs = jnp.log(factors)
    forward_sum = jnp.cumsum(logs[0], axis=-1)
    backward_sum = jnp.cumsum(logs[1][:, ::-1], axis=-1)[:, ::-1]
    totals = jnp.stack([forward_sum, backward_sum])
    positions = lax.broadcasted_iota(jnp.int32, (cells, cells), 0)
    columns = lax.broadcasted_iota(jnp.int32, (cells, cells), 1)
    lower = positions >= columns
    mask = jnp.stack([lower, columns >= positions])[:, None]
    spread = totals[..., :, None] - totals[..., None, :]
    transfer = jnp.where(mask, jnp.exp(jnp.where(mask, spread, 0.0)), 0.0)
    local = jnp.einsum("dvij,dvjc->dvic", transfer, source, precision=lax.Precision.HIGHEST)
    reach = jnp.exp(totals)
    pass_forward = reach[0][:, -1]
    pass_backward = reach[1][:, 0]
    leave_forward = local[0][:, -1, :]
    leave_backward = local[1][:, 0, :]
    length = lax.axis_size("gx")
    enter_forward = jnp.zeros_like(leave_forward)
    enter_backward = jnp.zeros_like(leave_backward)
    for step in range(length - 1):
        enter_forward = shifted(pass_forward[:, None] * enter_forward + leave_forward, "gx", 1)
        enter_backward = shifted(pass_backward[:, None] * enter_backward + leave_backward, "gx", -1)
    incoming = jnp.stack([enter_forward, enter_backward])
    swept = local + reach[..., None] * incoming[:, :, None, :]
    partial_moments = jnp.einsum("kdv,dvxc->kxc", weights, swept, precision=lax.Precision.HIGHEST)
    moments = lax.psum(partial_moments, "vert")
    moments = smooth_whole(moments)
    equil = equilibrium(
        moments,
        velocity[0][:, :, None, None],
        velocity[1][:, :, None, None],
        velocity[2][:, :, None, None],
    )
    updated = swept + relax[:, :, None, None] * (equil - swept)
    return (
        updated.reshape(2, vel_dev, cells * plane),
        moments.reshape(moments.shape[0], cells * plane),
    )


def solution(mesh):
    return jax.shard_map(
        per_device,
        mesh=mesh,
        in_specs=(
            P(None, "vert", "gx"),
            P(None, "vert", "gx"),
            P(None, None, "vert"),
            P(None, None, "vert"),
            P(None, "vert"),
        ),
        out_specs=(P(None, "vert", "gx"), P(None, "gx")),
        check_vma=False,
    )
```

profile of v0, /device:TPU:8, one launch (start us, length us, event | category | flops | bytes accessed | tf_op | source)
XLA Modules:
  0.0 295.8 jit_solution(12187332233541630807)
XLA Ops:
  7.2 0.0 all-reduce.2.cloned.1.call-start
  7.2 5.5 %reshape.142 = f32[2,64,32,192]{3,2,1,0:T(8,128)} reshape(f32[2,64,6144]{2,1,0:T(8,128)} %param.5) | data formatting | bytes 6291456 | tf_op jit(solution)/shard_map/reshape | solution.py:83
  12.8 0.1 copy.23
  12.9 0.1 copy.22
  13.0 0.2 reduce_window_sum.18
  13.2 0.1 rev.7
  13.2 0.1 copy.21
  13.3 0.2 reduce_window_sum.17
  13.6 6.2 %fusion.27 = f32[2,64,32,192]{3,2,1,0:T(8,128)S(1)} fusion(f32[2,64,32,192]{3,2,1,0:T(8,128)} %reshape.142, f32[2,64,32]{2,1,0:T(8,128)S(1)} %copy.23, f32[2,64,32]{2,1,0:T(8,128)S(1)} %get-tuple-element.27, pred[2,32,32]{2,1,0:T(8,128)(4,1)S(1)} %pad_add_fusion), kind=kOutput, calls=%fused_computation.40 | convolution fusion | flops 303169536 | bytes 6326272 | tf_op jit(solution)/shard_map/dvij,dvjc->dvic/dot_general | solution.py:95
  19.7 0.6 fusion.91
  20.4 0.1 slice_reduce_fusion
  20.5 0.1 bitcast_add_fusion.2
  20.6 1.3 collective-permute-start.3
  21.9 1.2 copy.121
  23.1 0.2 slice_reduce_fusion.1
  23.3 0.1 fusion.59
  23.4 4.5 %collective-permute-start = (f32[64,192]{1,0:T(8,128)S(1)}, f32[64,192]{1,0:T(8,128)S(1)}, u32[]{:S(2)}, u32[]{:S(2)}) collective-permute-start(f32[64,192]{1,0:T(8,128)S(1)} %fusion.59), channel_id=1, source_target_pairs={{0,64},{64,128},{128,192},{1,65},{65,129},{129,193},{2,66},{66,130... | collective-permute-start | bytes 147464 | tf_op jit(solution)/shard_map/ppermute | solution.py:32
  27.9 0.1 bitcast_add_fusion.1
  28.0 1.3 collective-permute-start.4
  29.3 0.5 collective-permute-done
  29.8 0.1 multiply_add_fusion.2
  29.9 4.3 %collective-permute-start.1 = (f32[64,192]{1,0:T(8,128)S(1)}, f32[64,192]{1,0:T(8,128)S(1)}, u32[]{:S(2)}, u32[]{:S(2)}) collective-permute-start(f32[64,192]{1,0:T(8,128)S(1)} %multiply_add_fusion.2), channel_id=1, source_target_pairs={{0,64},{64,128},{128,192},{1,65},{65,129},{129,193},{2,66},{66,130... | collective-permute-start | bytes 147464 | tf_op jit(solution)/shard_map/ppermute | solution.py:32
  34.2 0.0 collective-permute-done.4
  34.2 0.1 bitcast_add_fusion
  34.3 1.3 collective-permute-start.5
  35.5 0.5 collective-permute-done.1
  36.0 0.1 multiply_add_fusion.1
  36.1 4.3 %collective-permute-start.2 = (f32[64,192]{1,0:T(8,128)S(1)}, f32[64,192]{1,0:T(8,128)S(1)}, u32[]{:S(2)}, u32[]{:S(2)}) collective-permute-start(f32[64,192]{1,0:T(8,128)S(1)} %multiply_add_fusion.1), channel_id=1, source_target_pairs={{0,64},{64,128},{128,192},{1,65},{65,129},{129,193},{2,66},{66,130... | collective-permute-start | bytes 147464 | tf_op jit(solution)/shard_map/ppermute | solution.py:32
  40.4 0.0 collective-permute-done.5
  40.4 1.9 collective-permute-done.2
  42.3 0.0 copy-start.2
  42.3 0.7 multiply_add_fusion
  43.0 0.0 copy-start.3
  43.1 5.4 %fusion.34 = f32[13,32,192]{2,0,1:T(8,128)} fusion(f32[2,64,32,192]{3,2,1,0:T(8,128)S(1)} %multiply_add_fusion, f32[13,2,64]{2,1,0:T(2,128)S(1)} %copy-done.2), kind=kOutput, calls=%fused_computation.49 | convolution fusion | flops 122683392 | bytes 3471872 | tf_op jit(solution)/shard_map/kdv,dvxc->kxc/dot_general | solution.py:109
  48.5 0.0 all-reduce.2.cloned.1.call-update
  48.5 187.0 %all-reduce.2.cloned.1.call-done = f32[13,32,192]{2,0,1:T(8,128)} async-done(((f32[13,32,192]{2,0,1:T(8,128)}), f32[13,32,192]{2,0,1:T(8,128)}) %all-reduce.2.cloned.1.call-update) | async-done | bytes 319504 | tf_op jit(solution)/shard_map/psum | solution.py:110
  235.5 0.7 fusion.95
  236.3 3.4 %collective-permute-start.7 = (f32[13,1,192]{2,0,1:T(8,128)S(1)}, f32[13,1,192]{2,0,1:T(8,128)S(1)}, u32[]{:S(2)}, u32[]{:S(2)}) collective-permute-start(f32[13,1,192]{2,0,1:T(8,128)S(1)} %get-tuple-element.15), channel_id=1, source_target_pairs={{0,64},{64,128},{128,192},{1,65},{65,129},{129,193},{2,66},{66,130... | collective-permute-start | bytes 29960 | tf_op jit(solution)/shard_map/ppermute | solution.py:20
  239.6 1.3 collective-permute-start.6
  240.9 1.0 slice.214
  242.0 3.3 %collective-permute-done.6 = f32[13,1,192]{2,0,1:T(8,128)S(1)} collective-permute-done((f32[13,1,192]{2,0,1:T(8,128)S(1)}, f32[13,1,192]{2,0,1:T(8,128)S(1)}, u32[]{:S(2)}, u32[]{:S(2)}) %collective-permute-start.6) | collective-permute-done | bytes 10016 | tf_op jit(solution)/shard_map/ppermute | solution.py:22
  245.3 1.6 fusion.55
  246.9 0.0 copy-start.4
  246.9 3.4 %collective-permute-start.9 = (f32[13,1,192]{2,0,1:T(8,128)S(1)}, f32[13,1,192]{2,0,1:T(8,128)S(1)}, u32[]{:S(2)}, u32[]{:S(2)}) collective-permute-start(f32[13,1,192]{2,0,1:T(8,128)S(1)} %get-tuple-element.13), channel_id=1, source_target_pairs={{0,64},{64,128},{128,192},{1,65},{65,129},{129,193},{2,66},{66,130... | collective-permute-start | bytes 29960 | tf_op jit(solution)/shard_map/ppermute | solution.py:20
  250.3 1.3 collective-permute-start.8
  251.7 0.1 collective-permute-done.9
  251.8 4.2 %collective-permute-done.8 = f32[13,1,192]{2,0,1:T(8,128)S(1)} collective-permute-done((f32[13,1,192]{2,0,1:T(8,128)S(1)}, f32[13,1,192]{2,0,1:T(8,128)S(1)}, u32[]{:S(2)}, u32[]{:S(2)}) %collective-permute-start.8) | collective-permute-done | bytes 10016 | tf_op jit(solution)/shard_map/ppermute | solution.py:22
  256.0 0.1 fusion.51
  256.1 3.1 %collective-permute-start.11 = (f32[13,1,192]{2,0,1:T(8,128)S(1)}, f32[13,1,192]{2,0,1:T(8,128)S(1)}, u32[]{:S(2)}, u32[]{:S(2)}) collective-permute-start(f32[13,1,192]{2,0,1:T(8,128)S(1)} %get-tuple-element.11), channel_id=1, source_target_pairs={{0,64},{64,128},{128,192},{1,65},{65,129},{129,193},{2,66},{66,130... | collective-permute-start | bytes 29960 | tf_op jit(solution)/shard_map/ppermute | solution.py:20
  259.2 1.3 collective-permute-start.10
  260.5 0.1 collective-permute-done.11
  260.6 4.2 %collective-permute-done.10 = f32[13,1,192]{2,0,1:T(8,128)S(1)} collective-permute-done((f32[13,1,192]{2,0,1:T(8,128)S(1)}, f32[13,1,192]{2,0,1:T(8,128)S(1)}, u32[]{:S(2)}, u32[]{:S(2)}) %collective-permute-start.10) | collective-permute-done | bytes 10016 | tf_op jit(solution)/shard_map/ppermute | solution.py:22
  264.9 0.1 fusion.47
  265.0 1.9 collective-permute-start.13
  266.9 1.5 collective-permute-start.12
  268.4 4.1 %collective-permute-done.12 = f32[13,1,192]{2,0,1:T(8,128)S(1)} collective-permute-done((f32[13,1,192]{2,0,1:T(8,128)S(1)}, f32[13,1,192]{2,0,1:T(8,128)S(1)}, u32[]{:S(2)}, u32[]{:S(2)}) %collective-permute-start.12) | collective-permute-done | bytes 10016 | tf_op jit(solution)/shard_map/ppermute | solution.py:22
  272.6 0.1 fusion.43
  272.7 0.2 fusion.62
  272.9 0.3 copy.31
  273.3 0.9 reshape.144
  274.2 0.1 fusion.97
  274.3 0.1 fusion.96
  274.6 9.1 %fusion.24 = f32[2,64,32,192]{3,2,1,0:T(8,128)} fusion(f32[32,192]{1,0:T(8,128)S(1)} %bitcast.101, f32[32,192]{1,0:T(8,128)S(1)} %get-tuple-element.30, f32[32,192]{1,0:T(8,128)S(1)} %bitcast.102, f32[32,192]{1,0:T(8,128)S(1)} %bitcast.103, f32[32,192]{1,0:T(8,128)S(1)} %bitcast.104, f32[32,192]{1,0:T(8,128)S(1)} %bitcast.105, f32[32,192]{1,0:T(8,128)S(1)} %bitcast.106, ...), kind=kLoop, calls=%fused_computation.36 | loop fusion | flops 32243712 | bytes 6776832 | tf_op jit(solution)/shard_map/add | solution.py:118
  283.6 5.4 %reshape.143 = f32[2,64,6144]{2,1,0:T(8,128)} reshape(f32[2,64,32,192]{3,2,1,0:T(8,128)} %fusion.24) | data formatting | bytes 6291456 | tf_op jit(solution)/shard_map/reshape | solution.py:120
  (47 shorter events, 0.5 us)
Async XLA Ops:
  7.2 5.6 %copy-start.1 = (f32[2,64,32]{1,2,0:T(8,128)S(1)}, f32[2,64,32]{1,2,0:T(8,128)}, u32[]{:S(2)}) copy-start(f32[2,64,32]{1,2,0:T(8,128)} %param.6) | copy-start | bytes 49156
  7.2 228.4 %all-reduce.2.cloned.1.call-start = ((), (), s32[]{:S(2)}) async-start(), calls=%async_computation | async-start | bytes 1048576 | tf_op jit(solution)/shard_map/psum | solution.py:110
  19.7 22.6 %copy-start = (f32[2,64,32,192]{3,2,1,0:T(8,128)}, f32[2,64,32,192]{3,2,1,0:T(8,128)S(1)}, u32[]{:S(2)}) copy-start(f32[2,64,32,192]{3,2,1,0:T(8,128)S(1)} %fusion.27) | copy-start | bytes 9437188
  20.6 7.3 %collective-permute-start.3 = (f32[64,192]{1,0:T(8,128)S(1)}, f32[64,192]{1,0:T(8,128)S(1)}, u32[]{:S(2)}, u32[]{:S(2)}) collective-permute-start(f32[64,192]{1,0:T(8,128)S(1)} %bitcast_add_fusion.2), channel_id=1, source_target_pairs={{64,0},{128,64},{192,128},{65,1},{129,65},{193,129},{66,2},{130,66... | collective-permute-start | bytes 147464 | tf_op jit(solution)/shard_map/ppermute | solution.py:32
  23.4 6.4 %collective-permute-start = (f32[64,192]{1,0:T(8,128)S(1)}, f32[64,192]{1,0:T(8,128)S(1)}, u32[]{:S(2)}, u32[]{:S(2)}) collective-permute-start(f32[64,192]{1,0:T(8,128)S(1)} %fusion.59), channel_id=1, source_target_pairs={{0,64},{64,128},{128,192},{1,65},{65,129},{129,193},{2,66},{66,130... | collective-permute-start | bytes 147464 | tf_op jit(solution)/shard_map/ppermute | solution.py:32
  28.0 6.2 %collective-permute-start.4 = (f32[64,192]{1,0:T(8,128)S(1)}, f32[64,192]{1,0:T(8,128)S(1)}, u32[]{:S(2)}, u32[]{:S(2)}) collective-permute-start(f32[64,192]{1,0:T(8,128)S(1)} %bitcast_add_fusion.1), channel_id=1, source_target_pairs={{64,0},{128,64},{192,128},{65,1},{129,65},{193,129},{66,2},{130,66... | collective-permute-start | bytes 147464 | tf_op jit(solution)/shard_map/ppermute | solution.py:32
  29.9 6.2 %collective-permute-start.1 = (f32[64,192]{1,0:T(8,128)S(1)}, f32[64,192]{1,0:T(8,128)S(1)}, u32[]{:S(2)}, u32[]{:S(2)}) collective-permute-start(f32[64,192]{1,0:T(8,128)S(1)} %multiply_add_fusion.2), channel_id=1, source_target_pairs={{0,64},{64,128},{128,192},{1,65},{65,129},{129,193},{2,66},{66,130... | collective-permute-start | bytes 147464 | tf_op jit(solution)/shard_map/ppermute | solution.py:32
  34.3 6.2 %collective-permute-start.5 = (f32[64,192]{1,0:T(8,128)S(1)}, f32[64,192]{1,0:T(8,128)S(1)}, u32[]{:S(2)}, u32[]{:S(2)}) collective-permute-start(f32[64,192]{1,0:T(8,128)S(1)} %bitcast_add_fusion), channel_id=1, source_target_pairs={{64,0},{128,64},{192,128},{65,1},{129,65},{193,129},{66,2},{130,66... | collective-permute-start | bytes 147464 | tf_op jit(solution)/shard_map/ppermute | solution.py:32
  36.1 6.2 %collective-permute-start.2 = (f32[64,192]{1,0:T(8,128)S(1)}, f32[64,192]{1,0:T(8,128)S(1)}, u32[]{:S(2)}, u32[]{:S(2)}) collective-permute-start(f32[64,192]{1,0:T(8,128)S(1)} %multiply_add_fusion.1), channel_id=1, source_target_pairs={{0,64},{64,128},{128,192},{1,65},{65,129},{129,193},{2,66},{66,130... | collective-permute-start | bytes 147464 | tf_op jit(solution)/shard_map/ppermute | solution.py:32
  42.3 0.7 copy-start.2
  43.0 5.5 %copy-start.3 = (f32[3,2,64]{2,1,0:T(2,128)S(1)}, f32[3,2,64]{2,1,0:T(2,128)}, u32[]{:S(2)}) copy-start(f32[3,2,64]{2,1,0:T(2,128)} %param.7) | copy-start | bytes 4612
  236.3 5.7 %collective-permute-start.7 = (f32[13,1,192]{2,0,1:T(8,128)S(1)}, f32[13,1,192]{2,0,1:T(8,128)S(1)}, u32[]{:S(2)}, u32[]{:S(2)}) collective-permute-start(f32[13,1,192]{2,0,1:T(8,128)S(1)} %get-tuple-element.15), channel_id=1, source_target_pairs={{0,64},{64,128},{128,192},{1,65},{65,129},{129,193},{2,66},{66,130... | collective-permute-start | bytes 29960 | tf_op jit(solution)/shard_map/ppermute | solution.py:20
  239.6 5.6 %collective-permute-start.6 = (f32[13,1,192]{2,0,1:T(8,128)S(1)}, f32[13,1,192]{2,0,1:T(8,128)S(1)}, u32[]{:S(2)}, u32[]{:S(2)}) collective-permute-start(f32[13,1,192]{2,0,1:T(8,128)S(1)} %get-tuple-element.14), channel_id=1, source_target_pairs={{64,0},{128,64},{192,128},{65,1},{129,65},{193,129},{66,2},{130,66... | collective-permute-start | bytes 29960 | tf_op jit(solution)/shard_map/ppermute | solution.py:22
  246.9 27.7 %copy-start.4 = (f32[2,64]{1,0:T(2,128)S(1)}, f32[2,64]{1,0:T(2,128)}, u32[]{:S(2)}) copy-start(f32[2,64]{1,0:T(2,128)} %param.9) | copy-start | bytes 1540
  246.9 4.8 %collective-permute-start.9 = (f32[13,1,192]{2,0,1:T(8,128)S(1)}, f32[13,1,192]{2,0,1:T(8,128)S(1)}, u32[]{:S(2)}, u32[]{:S(2)}) collective-permute-start(f32[13,1,192]{2,0,1:T(8,128)S(1)} %get-tuple-element.13), channel_id=1, source_target_pairs={{0,64},{64,128},{128,192},{1,65},{65,129},{129,193},{2,66},{66,130... | collective-permute-start | bytes 29960 | tf_op jit(solution)/shard_map/ppermute | solution.py:20
  250.3 5.6 %collective-permute-start.8 = (f32[13,1,192]{2,0,1:T(8,128)S(1)}, f32[13,1,192]{2,0,1:T(8,128)S(1)}, u32[]{:S(2)}, u32[]{:S(2)}) collective-permute-start(f32[13,1,192]{2,0,1:T(8,128)S(1)} %get-tuple-element.12), channel_id=1, source_target_pairs={{64,0},{128,64},{192,128},{65,1},{129,65},{193,129},{66,2},{130,66... | collective-permute-start | bytes 29960 | tf_op jit(solution)/shard_map/ppermute | solution.py:22
  256.1 4.5 %collective-permute-start.11 = (f32[13,1,192]{2,0,1:T(8,128)S(1)}, f32[13,1,192]{2,0,1:T(8,128)S(1)}, u32[]{:S(2)}, u32[]{:S(2)}) collective-permute-start(f32[13,1,192]{2,0,1:T(8,128)S(1)} %get-tuple-element.11), channel_id=1, source_target_pairs={{0,64},{64,128},{128,192},{1,65},{65,129},{129,193},{2,66},{66,130... | collective-permute-start | bytes 29960 | tf_op jit(solution)/shard_map/ppermute | solution.py:20
  259.2 5.6 %collective-permute-start.10 = (f32[13,1,192]{2,0,1:T(8,128)S(1)}, f32[13,1,192]{2,0,1:T(8,128)S(1)}, u32[]{:S(2)}, u32[]{:S(2)}) collective-permute-start(f32[13,1,192]{2,0,1:T(8,128)S(1)} %get-tuple-element.10), channel_id=1, source_target_pairs={{64,0},{128,64},{192,128},{65,1},{129,65},{193,129},{66,2},{130,66... | collective-permute-start | bytes 29960 | tf_op jit(solution)/shard_map/ppermute | solution.py:22
  265.0 3.4 %collective-permute-start.13 = (f32[13,1,192]{2,0,1:T(8,128)S(1)}, f32[13,1,192]{2,0,1:T(8,128)S(1)}, u32[]{:S(2)}, u32[]{:S(2)}) collective-permute-start(f32[13,1,192]{2,0,1:T(8,128)S(1)} %get-tuple-element.9), channel_id=1, source_target_pairs={{0,64},{64,128},{128,192},{1,65},{65,129},{129,193},{2,66},{66,130... | collective-permute-start | bytes 29960 | tf_op jit(solution)/shard_map/ppermute | solution.py:20
  266.9 5.6 %collective-permute-start.12 = (f32[13,1,192]{2,0,1:T(8,128)S(1)}, f32[13,1,192]{2,0,1:T(8,128)S(1)}, u32[]{:S(2)}, u32[]{:S(2)}) collective-permute-start(f32[13,1,192]{2,0,1:T(8,128)S(1)} %get-tuple-element.8), channel_id=1, source_target_pairs={{64,0},{128,64},{192,128},{65,1},{129,65},{193,129},{66,2},{130,66... | collective-permute-start | bytes 29960 | tf_op jit(solution)/shard_map/ppermute | solution.py:22
Sparse Core Ops, SparseCore 0:
  48.6 186.8 all-reduce.1
where the time goes:
time: 297 us; the launch traced here: 296 us
  waiting for transfers between devices  206 us (69%)
  starting transfers between devices  34.1 us (11%)
  local copies, waits for them, and re-layouts  16.4 us (6%)
  between operations  14.6 us (5%)
  other arithmetic  13.1 us (4%)
  matrix products  11.6 us (4%)
    psum x1, waiting for transfers between devices, per_device(): moments = lax.psum(partial_moments, 'vert')  187 us
    ppermute x6, starting transfers between devices, shifted(): lax.ppermute(value, axis, [(source, source + steps) for source in range(l...  16.9 us
    ppermute x4, waiting for transfers between devices, padded_2(): lax.ppermute(head, axis, [((i + 1) % count, i) for i in range(ends)])  15.9 us
    ppermute x4, starting transfers between devices, padded_2(): lax.ppermute(tail, axis, [(i, (i + 1) % count) for i in range(ends)])  11.7 us
    add x1, other arithmetic, per_device(): updated = swept + relax[:, :, None, None] * (equil - swept)  9.05 us
    dot_general x1, matrix products, per_device(): jnp.einsum('dvij,dvjc->dvic', transfer, source, precision=lax.Precision.H...  6.16 us
  transfers between devices with their start and end apart: 15, of which 10 were waited for; matrix products, arithmetic and copies ran while one was open for 1% of the time, Pallas kernels for 0%

commit v1 on v0

v1 whole, which is shorter than its diff:
```python
import functools

import jax
import jax.numpy as jnp
from jax import lax
from jax.experimental import pallas as pl
from jax.experimental.pallas import tpu as pltpu
from jax.sharding import PartitionSpec as P

MESH = pl.DeviceIdType.MESH
F32, BF16 = jnp.float32, jnp.bfloat16
SMOOTH_RATE = 0.24
LOG2E = 1.4426950408889634

NX, NY, NZ = 4, 4, 8
TILES, SLOT = 48, 6
SLOT_ROWS = SLOT * 16
GROUPS = 2

XF, CR = 0, 6 * GROUPS
YR = CR + 4
ZR = YR + 3
ZG = ZR + 7
YG = ZG + 7
CG = YG + 3
HALO = CG + 5
N_SEM = HALO + 4


def kernel(
    dist, fac, vel, wgt, rel, out, mac,
    val, reach, snd, rcv, inc, wmat, phi, phit, coef_f, coef_l,
    stage, part, got_c, got_y, got_z, full, tmp, ld_sem, st_sem, ssem, rsem,
):
    gx = lax.axis_index("gx")
    vert = lax.axis_index("vert")
    y = vert // 16
    z = (vert // 2) % 8
    core = vert % 2

    def vert_of(y_, z_, core_):
        return y_ * 16 + z_ * 2 + core_

    def copy(src, dst, send, recv, x_, v_):
        return pltpu.make_async_remote_copy(
            src_ref=src, dst_ref=dst, send_sem=ssem.at[send], recv_sem=rsem.at[recv],
            device_id=(x_, v_), device_id_type=MESH,
        )

    def rows8(r):
        return pl.ds(pl.multiple_of(r * 8, 8), 8)

    def load(r):
        return pltpu.make_async_copy(dist.at[:, rows8(r), :], val.at[:, rows8(r), :], ld_sem.at[r])

    for r in range(8):
        load(r).start()

    barrier = pltpu.get_barrier_semaphore()

    def greet(x_, v_):
        pl.semaphore_signal(barrier, inc=1, device_id=(x_, v_), device_id_type=MESH)

    for t in range(1, NX):
        greet((gx + t) % NX, vert)
    greet(gx, vert_of(y, z, 1 - core))
    for t in range(1, NY):
        greet(gx, vert_of((y + t) % NY, z, core))
    for t in range(1, NZ):
        greet(gx, vert_of(y, (z + t) % NZ, core))
    has_left, has_right = gx > 0, gx < NX - 1
    halo_here = jnp.where(core == 1, has_left, has_right)
    halo_x = jnp.where(core == 1, gx - 1, gx + 1)
    halo_y = jnp.where(core == 1, NY - 1, 0)

    @pl.when(halo_here & (y != halo_y))
    def _():
        greet(halo_x, vert_of(halo_y, z, core))

    halo_source = ((core == 1) & (y == NY - 1) & has_right) | ((core == 0) & (y == 0) & has_left)

    lane = lax.broadcasted_iota(jnp.int32, (8, 128), 1)
    low = lane < 64

    def lanes2(a, b):
        return jnp.concatenate([a, b], axis=1)

    wide = jnp.zeros((16, 128), F32)
    wmat[...] = jnp.zeros_like(wmat)
    for k in range(13):
        row = lanes2(wgt[k, 0:1, :], wgt[k, 1:2, :])
        hi = row.astype(BF16).astype(F32)
        lo = row - hi
        wmat[k : k + 1, 0:128] = hi
        wmat[k : k + 1, 128:256] = hi
        wmat[16 + k : 17 + k, 0:128] = lo

    vx, vy, vz = [lanes2(vel[j, 0:1, :], vel[j, 1:2, :]) for j in range(3)]
    relax = lanes2(rel[0:1, :], rel[1:2, :])
    xx, yy, zz = vx * vx, vy * vy, vz * vz
    sq = xx + yy + zz
    one = jnp.ones_like(vx)
    feats = [vx * sq, vy * sq, vz * sq, xx, yy, zz, vx * vy, vx * vz, vy * vz, vx, vy, vz, one]
    phi[...] = jnp.zeros_like(phi)
    for n, feat in enumerate(feats):
        for base, f in ((0, feat * relax), (48, feat)):
            hi = f.astype(BF16).astype(F32)
            phi[base + n : base + n + 1, :] = hi
            phi[base + 16 + n : base + 17 + n, :] = hi
            phi[base + 32 + n : base + 33 + n, :] = f - hi
    phi[96:97, :] = 1.0 - relax
    phit[...] = phi[...].T

    def sweep(r, direction):
        rows = rows8(r)
        f = fac[direction, rows, :]
        q = jnp.sqrt(1.0 - f * f)

        def cols(t):
            return pl.ds(t * 128, 128)

        def spread(x, i):
            return jnp.broadcast_to(x[:, i : i + 1], (8, 128))

        zero = jnp.zeros((8, 128), F32)
        ones = jnp.ones((8, 128), F32)
        if direction == 0:
            f_prev = ones
            roll_a = roll_b = zero
            value = [zero] * 3
            total = [ones] * 3
            for p in range(16):
                fa, fc = spread(f, 2 * p), spread(f, 2 * p + 1)
                qa, qc = spread(q, 2 * p), spread(q, 2 * p + 1)
                ga, gc = fa * f_prev, fc * fa
                fs = [fa, jnp.where(low, fa, fc), fc]
                qs = [qa, jnp.where(low, qa, qc), qc]
                gs = [ga, jnp.where(low, ga, gc), gc]
                for j in range(3):
                    t = 3 * p + j
                    s = qs[j] * val[0, rows, cols(t)]
                    before = jnp.where(low, roll_a, roll_b)
                    roll_a, roll_b = roll_b, pltpu.roll(s, 64, 1)
                    value[j] = gs[j] * value[j] + (s + fs[j] * before)
                    total[j] = gs[j] * total[j]
                    val[0, rows, cols(t)] = value[j]
                    reach[0, rows, cols(t)] = total[j]
                f_prev = fc
            snd[0, rows, 0:128] = jnp.where(low, total[2], value[1])
            snd[0, rows, 128:256] = value[2]
        else:
            f_next = ones
            roll_a = roll_b = zero
            value = [zero] * 3
            total = [ones] * 3
            for p in range(15, -1, -1):
                fa, fc = spread(f, 2 * p), spread(f, 2 * p + 1)
                qa, qc = spread(q, 2 * p), spread(q, 2 * p + 1)
                ga, gc = fa * fc, fc * f_next
                fs = [fa, jnp.where(low, fa, fc), fc]
                qs = [qa, jnp.where(low, qa, qc), qc]
                gs = [ga, jnp.where(low, ga, gc), gc]
                for j in (2, 1, 0):
                    t = 3 * p + j
                    s = qs[j] * val[1, rows, cols(t)]
                    after = jnp.where(low, roll_b, roll_a)
                    roll_a, roll_b = roll_b, pltpu.roll(s, 64, 1)
                    value[j] = gs[j] * value[j] + (s + fs[j] * after)
                    total[j] = gs[j] * total[j]
                    val[1, rows, cols(t)] = value[j]
                    reach[1, rows, cols(t)] = total[j]
                f_next = fa
            snd[1, rows, 0:128] = value[0]
            snd[1, rows, 128:256] = jnp.where(low, value[1], total[0])

    def edge(direction, t, g, target):
        span = pl.ds(g * (64 // GROUPS), 64 // GROUPS)
        n = XF + (direction * 3 + t - 1) * GROUPS + g
        return copy(snd.at[direction, span, :], rcv.at[direction, t - 1, span, :], n, n, target, vert)

    for g in range(GROUPS):
        def sweep_rows(r, _):
            load(r).wait()
            sweep(r, 0)
            sweep(r, 1)
            return 0

        lax.fori_loop(g * 8 // GROUPS, (g + 1) * 8 // GROUPS, sweep_rows, 0)
        if g == 0:
            pl.semaphore_wait(barrier, 14 + jnp.where(halo_source, 3, 0))

        for t in range(1, NX):
            @pl.when(gx + t < NX)
            def _():
                edge(0, t, g, gx + t).start()

            @pl.when(gx - t >= 0)
            def _():
                edge(1, t, g, gx - t).start()

    for t in range(1, NX):
        for g in range(GROUPS):
            @pl.when(gx - t >= 0)
            def _():
                edge(0, t, g, (gx - t) % NX).wait_recv()

            @pl.when(gx + t < NX)
            def _():
                edge(1, t, g, (gx + t) % NX).wait_recv()

    def enter(r, _):
        rows = rows8(r)
        zero = jnp.zeros((8, 128), F32)

        def forward(n, state):
            a, b = state
            ra, rb = rcv[0, gx - n - 1, rows, 0:128], rcv[0, gx - n - 1, rows, 128:256]
            through = jnp.broadcast_to(ra[:, 0:1], (8, 128))
            return through * a + ra, through * b + rb

        a, b = lax.fori_loop(0, gx, forward, (zero, zero))
        ra, rb = pltpu.roll(a, 64, 1), pltpu.roll(b, 64, 1)
        inc[0, rows, 0:128] = jnp.where(low, ra, rb)
        inc[0, rows, 128:256] = jnp.where(low, rb, a)
        inc[0, rows, 256:384] = b

        def backward(n, state):
            a, b = state
            last = NX - 2 - gx - n
            ra, rb = rcv[1, last, rows, 0:128], rcv[1, last, rows, 128:256]
            through = jnp.broadcast_to(rb[:, 127:128], (8, 128))
            return through * a + ra, through * b + rb

        a, b = lax.fori_loop(0, NX - 1 - gx, backward, (zero, zero))
        ra, rb = pltpu.roll(a, 64, 1), pltpu.roll(b, 64, 1)
        inc[1, rows, 0:128] = a
        inc[1, rows, 128:256] = jnp.where(low, b, ra)
        inc[1, rows, 256:384] = jnp.where(low, ra, rb)
        return 0

    lax.fori_loop(0, 8, enter, 0)

    weights = wmat[...].astype(BF16)

    def moments(slot, dst, dst_row):
        for half in range(2):
            cols = pl.ds(pl.multiple_of(slot * 768 + half * 384, 128), 384)
            swept = val[:, :, cols] + reach[:, :, cols] * inc[...]
            val[:, :, cols] = swept
            flat = swept.reshape(128, 384)
            hi = flat.astype(BF16)
            lo = (flat - hi.astype(F32)).astype(BF16)
            both = jnp.dot(weights, jnp.concatenate([hi, lo], axis=0), preferred_element_type=F32)
            total = both[0:16] + both[16:32]
            for j in range(3):
                dst[pl.ds(pl.multiple_of(dst_row + (half * 3 + j) * 16, 16), 16), :] = total[:, j * 128 : (j + 1) * 128]

    def slot_rows(n):
        return pl.ds(pl.multiple_of(n * SLOT_ROWS, SLOT_ROWS), SLOT_ROWS)

    partner = vert_of(y, z, 1 - core)

    def to_core(n):
        return copy(stage.at[slot_rows(n), :], got_c.at[slot_rows(n), :], CR + n, CR + n, gx, partner)

    def other_half(n, _):
        moments((1 - core) * 4 + (y + n + 1) % NY, stage, n * SLOT_ROWS)
        to_core(n).start()
        return 0

    lax.fori_loop(0, 4, other_half, 0)

    def to_y(n):
        return copy(
            part.at[slot_rows(n), :], got_y.at[slot_rows(n), :], YR + n, YR + n, gx, vert_of((y + n + 1) % NY, z, core)
        )

    def own_half(n, _):
        moments(core * 4 + (y + n + 1) % NY, part, n * SLOT_ROWS)
        to_core(n).wait_recv()
        part[slot_rows(n), :] += got_c[slot_rows(n), :]

        @pl.when(n < 3)
        def _():
            to_y(n).start()

        return 0

    lax.fori_loop(0, 4, own_half, 0)
    for n in range(3):
        to_y(n).wait_recv()
        part[slot_rows(3), :] += got_y[slot_rows(n), :]

    def tile_rows(n):
        return pl.ds(pl.multiple_of(n * 16, 16), 16)

    mine = core * 4 + y
    own_row = (1 + mine) * SLOT_ROWS

    def to_z(n):
        peer = (z + n + 1) % NZ
        return copy(
            part.at[pl.ds(pl.multiple_of(3 * SLOT_ROWS + peer * 16, 16), 16), :], got_z.at[tile_rows(n), :],
            ZR + n, ZR + n, gx, vert_of(y, peer, core),
        )

    def from_owner(n, owner, target):
        tile = pl.ds(pl.multiple_of(own_row + owner * 16, 16), 16)
        return copy(full.at[tile, :], full.at[tile, :], ZG + n, ZG + n, gx, vert_of(y, target, core))

    for n in range(7):
        @pl.when((z + n + 1) % NZ < SLOT)
        def _():
            to_z(n).start()

    @pl.when(z < SLOT)
    def _():
        total = part[pl.ds(pl.multiple_of(3 * SLOT_ROWS + z * 16, 16), 16), :]
        for n in range(7):
            copy(got_z.at[tile_rows(n), :], got_z.at[tile_rows(n), :], ZR + n, ZR + n, gx, vert).wait_recv()
            total += got_z[tile_rows(n), :]
        full[pl.ds(pl.multiple_of(own_row + z * 16, 16), 16), :] = total
        for n in range(7):
            from_owner(n, z, (z + n + 1) % NZ).start()

    for n in range(7):
        owner = (z + NZ - n - 1) % NZ

        @pl.when(owner < SLOT)
        def _():
            from_owner(n, owner, z).wait_recv()

    def slot_of(n):
        return pl.ds(pl.multiple_of((1 + n) * SLOT_ROWS, SLOT_ROWS), SLOT_ROWS)

    def gather_y(n, slot):
        return copy(
            full.at[slot_of(slot), :], full.at[slot_of(slot), :], YG + n, YG + n, gx, vert_of((y + n + 1) % NY, z, core)
        )

    halo_slot = jnp.where(core == 1, -1, 8)

    def send_halo(n):
        return copy(
            full.at[slot_of(mine), :], full.at[slot_of(halo_slot), :], HALO + n, HALO,
            jnp.where(core == 1, gx + 1, gx - 1), vert_of((y + n) % NY, z, core),
        )

    def gather_core(n, slot):
        return copy(full.at[slot_of(slot), :], full.at[slot_of(slot), :], CG + n, CG + n, gx, partner)

    for n in range(3):
        gather_y(n, mine).start()

    @pl.when(halo_source)
    def _():
        for n in range(4):
            send_halo(n).start()

    gather_core(3, mine).start()
    for n in range(3):
        slot = core * 4 + (y + NY - n - 1) % NY
        gather_y(n, slot).wait_recv()
        gather_core(n, slot).start()

    @pl.when(halo_here)
    def _():
        copy(full.at[slot_of(halo_slot), :], full.at[slot_of(halo_slot), :], HALO, HALO, gx, vert).wait_recv()
        gather_core(4, halo_slot).start()

    nothing = jnp.zeros((SLOT_ROWS, 128), F32)

    @pl.when(jnp.logical_not(has_left))
    def _():
        full[slot_of(-1), :] = nothing

    @pl.when(jnp.logical_not(has_right))
    def _():
        full[slot_of(8), :] = nothing

    for n in range(4):
        gather_core(n, (1 - core) * 4 + (y + NY - n - 1) % NY).wait_recv()

    other_halo = jnp.where(core == 1, 8, -1)

    @pl.when(jnp.where(core == 1, has_right, has_left))
    def _():
        gather_core(4, other_halo).wait_recv()

    for n in range(3):
        gather_y(n, mine).wait_send()

    @pl.when(halo_source)
    def _():
        for n in range(4):
            send_halo(n).wait_send()

    for n in range(4):
        gather_core(n, core * 4 + (y + NY - n - 1) % NY).wait_send()

    @pl.when(halo_here)
    def _():
        gather_core(4, halo_slot).wait_send()

    @pl.when(z < SLOT)
    def _():
        for n in range(7):
            from_owner(n, z, (z + n + 1) % NZ).wait_send()

    left_flag = jnp.where(has_left, 1.0, 0.0).astype(F32)
    right_flag = jnp.where(has_right, 1.0, 0.0).astype(F32)

    def smooth(src, dst, first, last):
        def get(t):
            if t < 0 or t > 59:
                return [jnp.zeros((8, 128), F32)] * 2
            return [src[t * 16 + 8 * h : t * 16 + 8 * h + 8, :] for h in range(2)]

        def rolled(t):
            return [pltpu.roll(m, 64, 1) for m in get(t)]

        around = {t: rolled(t) for t in range(first - 2, first + 2)}
        for t in range(first, last + 1):
            around[t + 2] = rolled(t + 2)
            here = get(t)
            density = jnp.broadcast_to(here[0][0:1, :], (8, 128))
            coef = SMOOTH_RATE / (1.0 + density * density)
            if t < SLOT:
                coef = coef * left_flag
            if t >= 54:
                coef = coef * right_flag
            for h in range(2):
                before = jnp.where(low, around[t - 2][h], around[t - 1][h])
                after = jnp.where(low, around[t + 1][h], around[t + 2][h])
                dst[t * 16 + 8 * h : t * 16 + 8 * h + 8, :] = here[h] + coef * (before + after - 2.0 * here[h])
            del around[t - 2]

    smooth(full, tmp, 1, 58)
    smooth(tmp, full, 3, 56)
    smooth(full, tmp, 4, 55)
    smooth(tmp, full, 6, 53)
    for t in range(TILES):
        mac[:, t * 128 : (t + 1) * 128] = full[(t + 6) * 16 : (t + 6) * 16 + 13, :]

    def row(k):
        return jnp.tanh(full[pl.ds(96 + k, TILES, stride=16), :])

    density = 1.0 + 0.5 * row(0)
    ux, uy, uz = 0.5 * row(1), 0.5 * row(2), 0.5 * row(3)
    g = 1.0 / (1.0 + 0.5 * row(4))
    s0, s1, s2, s3, s4 = [0.2 * row(5 + j) for j in range(5)]
    qx, qy, qz = [0.2 * row(10 + j) for j in range(3)]
    front = density * g * jnp.sqrt(g)
    h = 0.5 * g
    sxx, syy = 0.5 * s3, 0.5 * s4
    szz = -(sxx + syy)
    square = ux * ux + uy * uy + uz * uz
    a = qx * ux + qy * uy + qz * uz
    b = h * square - 2.5
    ah = a * h
    scale = front * g
    quad = (
        ux * (sxx * ux + s0 * uy + s1 * uz) + uy * (syy * uy + s2 * uz) + szz * uz * uz
    )
    values_f = [
        scale * h * qx, scale * h * qy, scale * h * qz,
        scale * (sxx - g * qx * ux - ah),
        scale * (syy - g * qy * uy - ah),
        scale * (szz - g * qz * uz - ah),
        scale * (s0 - g * (qx * uy + qy * ux)),
        scale * (s1 - g * (qx * uz + qz * ux)),
        scale * (s2 - g * (qy * uz + qz * uy)),
        scale * (b * qx + 2.0 * ah * ux - (2.0 * sxx * ux + s0 * uy + s1 * uz)),
        scale * (b * qy + 2.0 * ah * uy - (s0 * ux + 2.0 * syy * uy + s2 * uz)),
        scale * (b * qz + 2.0 * ah * uz - (s1 * ux + s2 * uy + 2.0 * szz * uz)),
        front + scale * (quad - a * b),
    ]
    le = -LOG2E * h
    none = jnp.zeros_like(le)
    values_l = [none] * 3 + [le] * 3 + [none] * 3 + [-2.0 * le * ux, -2.0 * le * uy, -2.0 * le * uz, le * square]
    for n in range(16):
        coef_f[pl.ds(n, TILES, stride=16), :] = values_f[n] if n < 13 else none
        coef_l[pl.ds(n, TILES, stride=16), :] = values_l[n] if n < 13 else none

    lhs_f = phit[:, 0:48].astype(BF16)
    lhs_l = phit[:, 48:96].astype(BF16)
    keep = jnp.broadcast_to(phit[:, 96:97], (128, 128))
    keep = jnp.concatenate([keep] * 3, axis=1)

    def split(ref, n):
        c = jnp.concatenate([ref[pl.ds(pl.multiple_of(n * 48 + 16 * j, 16), 16), :] for j in range(3)], axis=1)
        hi = c.astype(BF16)
        lo = (c - hi.astype(F32)).astype(BF16)
        return jnp.concatenate([hi, lo, hi], axis=0)

    def relaxed(n, _):
        cols = pl.ds(pl.multiple_of(n * 384, 128), 384)
        poly = jnp.dot(lhs_f, split(coef_f, n), preferred_element_type=F32)
        power = jnp.dot(lhs_l, split(coef_l, n), preferred_element_type=F32)
        swept = val[:, :, cols].reshape(128, 384)
        out[:, :, cols] = (keep * swept + poly * jnp.exp2(power)).reshape(2, 64, 384)
        return 0

    lax.fori_loop(0, 16, relaxed, 0)

    for g in range(GROUPS):
        for t in range(1, NX):
            @pl.when(gx + t < NX)
            def _():
                edge(0, t, g, (gx + t) % NX).wait_send()

            @pl.when(gx - t >= 0)
            def _():
                edge(1, t, g, (gx - t) % NX).wait_send()

    for n in range(4):
        to_core(n).wait_send()
    for n in range(3):
        to_y(n).wait_send()
    for n in range(7):
        @pl.when((z + n + 1) % NZ < SLOT)
        def _():
            to_z(n).wait_send()


def per_device(dist, factors, velocity, weights, relax):
    vmem = pl.BlockSpec(memory_space=pltpu.VMEM)
    return pl.pallas_call(
        kernel,
        out_shape=(
            jax.ShapeDtypeStruct((2, 64, 6144), F32),
            jax.ShapeDtypeStruct((13, 6144), F32),
        ),
        in_specs=[pl.BlockSpec(memory_space=pl.ANY), vmem, vmem, vmem, vmem],
        out_specs=(vmem, vmem),
        scratch_shapes=[
            pltpu.VMEM((2, 64, 6144), F32),
            pltpu.VMEM((2, 64, 6144), F32),
            pltpu.VMEM((2, 64, 256), F32),
            pltpu.VMEM((2, 3, 64, 256), F32),
            pltpu.VMEM((2, 64, 384), F32),
            pltpu.VMEM((32, 256), F32),
            pltpu.VMEM((128, 128), F32),
            pltpu.VMEM((128, 128), F32),
            pltpu.VMEM((TILES * 16, 128), F32),
            pltpu.VMEM((TILES * 16, 128), F32),
            pltpu.VMEM((4 * SLOT_ROWS, 128), F32),
            pltpu.VMEM((4 * SLOT_ROWS, 128), F32),
            pltpu.VMEM((4 * SLOT_ROWS, 128), F32),
            pltpu.VMEM((3 * SLOT_ROWS, 128), F32),
            pltpu.VMEM((7 * 16, 128), F32),
            pltpu.VMEM((10 * SLOT_ROWS, 128), F32),
            pltpu.VMEM((10 * SLOT_ROWS, 128), F32),
            pltpu.SemaphoreType.DMA((8,)),
            pltpu.SemaphoreType.DMA((8,)),
            pltpu.SemaphoreType.DMA((N_SEM,)),
            pltpu.SemaphoreType.DMA((N_SEM,)),
        ],
        compiler_params=pltpu.CompilerParams(
            collective_id=0, has_side_effects=True, vmem_limit_bytes=32 * 2**20
        ),
    )(dist, factors, velocity, weights, relax)


def solution(mesh):
    return jax.shard_map(
        per_device,
        mesh=mesh,
        in_specs=(
            P(None, "vert", "gx"),
            P(None, "vert", "gx"),
            P(None, None, "vert"),
            P(None, None, "vert"),
            P(None, "vert"),
        ),
        out_specs=(P(None, "vert", "gx"), P(None, "gx")),
        check_vma=False,
    )
```

time: 297 us -> 61.3 us (0.21)
  the two profiles are of different devices: /device:TPU:8 before, /device:TPU:1 now
where the time goes in v1:
time: 61.3 us; the launch traced here: 61 us
  Pallas kernels  53.2 us (87%)
  local copies, waits for them, and re-layouts  7.21 us (12%)
  between operations  0.65 us (1%)
    pallas_call x1, Pallas kernels, per_device(): pl.pallas_call(kernel, out_shape=(jax.ShapeDtypeStruct((2, 64, 6144), F32...  53.2 us
    unnamed x11, local copies, waits for them, and re-layouts  7.21 us

profile of v1, /device:TPU:1, one launch (start us, length us, event | category | flops | bytes accessed | tf_op | source)
XLA Modules:
  0.0 61.0 jit_solution(2766611438870466373)
XLA Ops:
  0.6 0.8 %copy.7.fac = f32[2,64,32]{2,1,0:T(8,128)S(1)} copy(f32[2,64,32]{1,2,0:T(8,128)} %param.6) | data formatting | bytes 32768 | tf_op args[1]
  1.5 0.0 copy-start
  1.5 1.9 %copy-done = f32[2,64,6144]{2,1,0:T(8,128)S(1)} copy-done((f32[2,64,6144]{2,1,0:T(8,128)S(1)}, f32[2,64,6144]{2,1,0:T(8,128)}, u32[]{:S(2)}) %copy-start) | copy-done | bytes 3145752
  3.4 0.0 copy-start.1
  3.4 0.7 %copy-done.1 = f32[13,2,64]{2,1,0:T(2,128)S(1)} copy-done((f32[13,2,64]{2,1,0:T(2,128)S(1)}, f32[13,2,64]{2,1,0:T(2,128)}, u32[]{:S(2)}) %copy-start.1) | copy-done | bytes 6680
  4.1 0.0 copy-start.2
  4.1 0.7 %copy-done.2 = f32[3,2,64]{2,1,0:T(2,128)S(1)} copy-done((f32[3,2,64]{2,1,0:T(2,128)S(1)}, f32[3,2,64]{2,1,0:T(2,128)}, u32[]{:S(2)}) %copy-start.2) | copy-done | bytes 1560
  4.8 0.0 copy-start.3
  4.8 0.7 %copy-done.3 = f32[2,64]{1,0:T(2,128)S(1)} copy-done((f32[2,64]{1,0:T(2,128)S(1)}, f32[2,64]{1,0:T(2,128)}, u32[]{:S(2)}) %copy-start.3) | copy-done | bytes 536
  5.4 53.2 %shard_map.68 = (f32[2,64,6144]{2,1,0:T(8,128)S(1)}, f32[13,6144]{1,0:T(8,128)S(1)}) custom-call(f32[2,64,6144]{2,1,0:T(8,128)S(1)} %copy-done, f32[2,64,32]{2,1,0:T(8,128)S(1)} %copy.7.fac, f32[3,2,64]{2,1,0:T(2,128)S(1)} %copy-done.2, f32[13,2,64]{2,1,0:T(2,128)S(1)} %copy-done.1, f32[2,64]{1,0:T(2,128)S(1)} %copy-done.3), custom_call_target="tpu_custom_call" | custom-call | tf_op jit(solution)/shard_map/pallas_call | solution.py:528
  58.6 1.7 %copy.10 = f32[2,64,6144]{2,1,0:T(8,128)} copy(f32[2,64,6144]{2,1,0:T(8,128)S(1)} %get-tuple-element.4) | data formatting | bytes 6291456
  60.3 0.7 %copy.11 = f32[13,6144]{1,0:T(8,128)} copy(f32[13,6144]{1,0:T(8,128)S(1)} %get-tuple-element.5) | data formatting | bytes 638976
Async XLA Ops:
  1.5 1.9 %copy-start = (f32[2,64,6144]{2,1,0:T(8,128)S(1)}, f32[2,64,6144]{2,1,0:T(8,128)}, u32[]{:S(2)}) copy-start(f32[2,64,6144]{2,1,0:T(8,128)} %dist.1) | copy-start | bytes 9437188
  3.4 0.7 %copy-start.1 = (f32[13,2,64]{2,1,0:T(2,128)S(1)}, f32[13,2,64]{2,1,0:T(2,128)}, u32[]{:S(2)}) copy-start(f32[13,2,64]{2,1,0:T(2,128)} %wgt.1) | copy-start | bytes 19972
  4.1 0.7 %copy-start.2 = (f32[3,2,64]{2,1,0:T(2,128)S(1)}, f32[3,2,64]{2,1,0:T(2,128)}, u32[]{:S(2)}) copy-start(f32[3,2,64]{2,1,0:T(2,128)} %vel.1) | copy-start | bytes 4612
  4.8 0.7 %copy-start.3 = (f32[2,64]{1,0:T(2,128)S(1)}, f32[2,64]{1,0:T(2,128)}, u32[]{:S(2)}) copy-start(f32[2,64]{1,0:T(2,128)} %rel.1) | copy-start | bytes 1540

commit v2 on v1

--- a/solution.py
+++ b/solution.py
@@ -16,6 +16,7 @@
 TILES, SLOT = 48, 6
 SLOT_ROWS = SLOT * 16
 GROUPS = 2
+BUFS = 4
 
 XF, CR = 0, 6 * GROUPS
 YR = CR + 4
@@ -28,9 +29,9 @@
 
 
 def kernel(
-    dist, fac, vel, wgt, rel, out, mac,
-    val, reach, snd, rcv, inc, wmat, phi, phit, coef_f, coef_l,
-    stage, part, got_c, got_y, got_z, full, tmp, ld_sem, st_sem, ssem, rsem,
+    dist, fac_hbm, vel_hbm, wgt_hbm, rel_hbm, val, moved, phit,
+    fac, vel, wgt, rel, lhs, reach, scaled, snd, rcv, inc, wmat, phi,
+    stage, part, got_c, got_y, got_z, full, tmp, ld_sem, small_sem, ssem, rsem,
 ):
     gx = lax.axis_index("gx")
     vert = lax.axis_index("vert")
@@ -53,6 +54,12 @@
     def load(r):
         return pltpu.make_async_copy(dist.at[:, rows8(r), :], val.at[:, rows8(r), :], ld_sem.at[r])
 
+    small = [
+        pltpu.make_async_copy(src, dst, small_sem.at[n])
+        for n, (src, dst) in enumerate(((fac_hbm, fac), (wgt_hbm, wgt), (vel_hbm, vel), (rel_hbm, rel)))
+    ]
+    for one_copy in small:
+        one_copy.start()
     for r in range(8):
         load(r).start()
 
@@ -85,7 +92,101 @@
     def lanes2(a, b):
         return jnp.concatenate([a, b], axis=1)
 
-    wide = jnp.zeros((16, 128), F32)
+    small[0].wait()
+    compact = lanes2(fac[0], fac[1])
+    for n, x in enumerate((compact, jnp.sqrt(1.0 - compact * compact))):
+        hi = x.astype(BF16).astype(F32)
+        mid = (x - hi).astype(BF16).astype(F32)
+        parts = jnp.concatenate([hi, mid, x - hi - mid, jnp.zeros_like(x)], axis=0)
+        lhs[n * 128 : (n + 1) * 128, :] = parts.T.astype(BF16)
+
+    def spread(p, _):
+        cell = lax.broadcasted_iota(jnp.int32, (96, 384), 0) % 32
+        second = lax.broadcasted_iota(jnp.int32, (96, 384), 1) >= 192
+        picks = jnp.where(cell == 2 * p + jnp.where(second, 1, 0), 1.0, 0.0).astype(BF16)
+        cols = pl.ds(pl.multiple_of(p * 384, 128), 384)
+        both = jnp.dot(lhs[:, 0:96], picks, preferred_element_type=F32)
+        reach[:, :, cols] = both[0:128].reshape(2, 64, 384)
+        scaled[:, :, cols] = both[128:256].reshape(2, 64, 384)
+        return 0
+
+    lax.fori_loop(0, 16, spread, 0)
+
+    def sweep(r):
+        rows = rows8(r)
+        zero = jnp.zeros((8, 128), F32)
+        ones = jnp.ones((8, 128), F32)
+
+        def cols(t):
+            return pl.ds(t * 128, 128)
+
+        value = [[zero] * 3, [zero] * 3]
+        total = [[ones] * 3, [ones] * 3]
+        rolls = [[zero, zero], [zero, zero]]
+        f_near = [ones, ones]
+        for step in range(16):
+            for d in range(2):
+                p = step if d == 0 else 15 - step
+                f = [reach[d, rows, cols(3 * p + j)] for j in range(3)]
+                first, second = (f[0], f[2]) if d == 0 else (f[2], f[0])
+                near, far = first * f_near[d], second * first
+                f_near[d] = second
+                if d == 0:
+                    gs = [near, jnp.where(low, near, far), far]
+                else:
+                    gs = [far, jnp.where(low, far, near), near]
+                for j in (0, 1, 2) if d == 0 else (2, 1, 0):
+                    t = 3 * p + j
+                    s = scaled[d, rows, cols(t)] * val[d, rows, cols(t)]
+                    two_off, one_off = rolls[d]
+                    neighbour = jnp.where(low, two_off, one_off) if d == 0 else jnp.where(low, one_off, two_off)
+                    rolls[d] = [one_off, pltpu.roll(s, 64, 1)]
+                    value[d][j] = gs[j] * value[d][j] + (s + f[j] * neighbour)
+                    total[d][j] = gs[j] * total[d][j]
+                    val[d, rows, cols(t)] = value[d][j]
+                    reach[d, rows, cols(t)] = total[d][j]
+        snd[0, rows, 0:128] = jnp.where(low, total[0][2], value[0][1])
+        snd[0, rows, 128:256] = value[0][2]
+        snd[1, rows, 0:128] = value[1][0]
+        snd[1, rows, 128:256] = jnp.where(low, value[1][1], total[1][0])
+
+    def edge(direction, t, g, target):
+        span = pl.ds(g * (64 // GROUPS), 64 // GROUPS)
+        n = XF + (direction * 3 + t - 1) * GROUPS + g
+        return copy(snd.at[direction, span, :], rcv.at[direction, t - 1, span, :], n, n, target, vert)
+
+    def drain_x():
+        for g in range(GROUPS):
+            for t in range(1, NX):
+                @pl.when(gx + t < NX)
+                def _():
+                    edge(0, t, g, (gx + t) % NX).wait_send()
+
+                @pl.when(gx - t >= 0)
+                def _():
+                    edge(1, t, g, (gx - t) % NX).wait_send()
+
+    for g in range(GROUPS):
+        def sweep_rows(r, _):
+            load(r).wait()
+            sweep(r)
+            return 0
+
+        lax.fori_loop(g * 8 // GROUPS, (g + 1) * 8 // GROUPS, sweep_rows, 0)
+        if g == 0:
+            pl.semaphore_wait(barrier, 14 + jnp.where(halo_source, 3, 0))
+
+        for t in range(1, NX):
+            @pl.when(gx + t < NX)
+            def _():
+                edge(0, t, g, gx + t).start()
+
+            @pl.when(gx - t >= 0)
+            def _():
+                edge(1, t, g, gx - t).start()
+
+    for one_copy in small[1:]:
+        one_copy.wait()
     wmat[...] = jnp.zeros_like(wmat)
     for k in range(13):
         row = lanes2(wgt[k, 0:1, :], wgt[k, 1:2, :])
@@ -111,93 +212,6 @@
     phi[96:97, :] = 1.0 - relax
     phit[...] = phi[...].T
 
-    def sweep(r, direction):
-        rows = rows8(r)
-        f = fac[direction, rows, :]
-        q = jnp.sqrt(1.0 - f * f)
-
-        def cols(t):
-            return pl.ds(t * 128, 128)
-
-        def spread(x, i):
-            return jnp.broadcast_to(x[:, i : i + 1], (8, 128))
-
-        zero = jnp.zeros((8, 128), F32)
-        ones = jnp.ones((8, 128), F32)
-        if direction == 0:
-            f_prev = ones
-            roll_a = roll_b = zero
-            value = [zero] * 3
-            total = [ones] * 3
-            for p in range(16):
-                fa, fc = spread(f, 2 * p), spread(f, 2 * p + 1)
-                qa, qc = spread(q, 2 * p), spread(q, 2 * p + 1)
-                ga, gc = fa * f_prev, fc * fa
-                fs = [fa, jnp.where(low, fa, fc), fc]
-                qs = [qa, jnp.where(low, qa, qc), qc]
-                gs = [ga, jnp.where(low, ga, gc), gc]
-                for j in range(3):
-                    t = 3 * p + j
-                    s = qs[j] * val[0, rows, cols(t)]
-                    before = jnp.where(low, roll_a, roll_b)
-                    roll_a, roll_b = roll_b, pltpu.roll(s, 64, 1)
-                    value[j] = gs[j] * value[j] + (s + fs[j] * before)
-                    total[j] = gs[j] * total[j]
-                    val[0, rows, cols(t)] = value[j]
-                    reach[0, rows, cols(t)] = total[j]
-                f_prev = fc
-            snd[0, rows, 0:128] = jnp.where(low, total[2], value[1])
-            snd[0, rows, 128:256] = value[2]
-        else:
-            f_next = ones
-            roll_a = roll_b = zero
-            value = [zero] * 3
-            total = [ones] * 3
-            for p in range(15, -1, -1):
-                fa, fc = spread(f, 2 * p), spread(f, 2 * p + 1)
-                qa, qc = spread(q, 2 * p), spread(q, 2 * p + 1)
-                ga, gc = fa * fc, fc * f_next
-                fs = [fa, jnp.where(low, fa, fc), fc]
-                qs = [qa, jnp.where(low, qa, qc), qc]
-                gs = [ga, jnp.where(low, ga, gc), gc]
-                for j in (2, 1, 0):
-                    t = 3 * p + j
-                    s = qs[j] * val[1, rows, cols(t)]
-                    after = jnp.where(low, roll_b, roll_a)
-                    roll_a, roll_b = roll_b, pltpu.roll(s, 64, 1)
-                    value[j] = gs[j] * value[j] + (s + fs[j] * after)
-                    total[j] = gs[j] * total[j]
-                    val[1, rows, cols(t)] = value[j]
-                    reach[1, rows, cols(t)] = total[j]
-                f_next = fa
-            snd[1, rows, 0:128] = value[0]
-            snd[1, rows, 128:256] = jnp.where(low, value[1], total[0])
-
-    def edge(direction, t, g, target):
-        span = pl.ds(g * (64 // GROUPS), 64 // GROUPS)
-        n = XF + (direction * 3 + t - 1) * GROUPS + g
-        return copy(snd.at[direction, span, :], rcv.at[direction, t - 1, span, :], n, n, target, vert)
-
-    for g in range(GROUPS):
-        def sweep_rows(r, _):
-            load(r).wait()
-            sweep(r, 0)
-            sweep(r, 1)
-            return 0
-
-        lax.fori_loop(g * 8 // GROUPS, (g + 1) * 8 // GROUPS, sweep_rows, 0)
-        if g == 0:
-            pl.semaphore_wait(barrier, 14 + jnp.where(halo_source, 3, 0))
-
-        for t in range(1, NX):
-            @pl.when(gx + t < NX)
-            def _():
-                edge(0, t, g, gx + t).start()
-
-            @pl.when(gx - t >= 0)
-            def _():
-                edge(1, t, g, gx - t).start()
-
     for t in range(1, NX):
         for g in range(GROUPS):
             @pl.when(gx - t >= 0)
@@ -291,6 +305,12 @@
         to_y(n).wait_recv()
         part[slot_rows(3), :] += got_y[slot_rows(n), :]
 
+    def drain_sums():
+        for n in range(4):
+            to_core(n).wait_send()
+        for n in range(3):
+            to_y(n).wait_send()
+
     def tile_rows(n):
         return pl.ds(pl.multiple_of(n * 16, 16), 16)
 
@@ -307,6 +327,12 @@
     def from_owner(n, owner, target):
         tile = pl.ds(pl.multiple_of(own_row + owner * 16, 16), 16)
         return copy(full.at[tile, :], full.at[tile, :], ZG + n, ZG + n, gx, vert_of(y, target, core))
+
+    def drain_z():
+        for n in range(7):
+            @pl.when((z + n + 1) % NZ < SLOT)
+            def _():
+                to_z(n).wait_send()
 
     for n in range(7):
         @pl.when((z + n + 1) % NZ < SLOT)
@@ -410,7 +436,7 @@
     left_flag = jnp.where(has_left, 1.0, 0.0).astype(F32)
     right_flag = jnp.where(has_right, 1.0, 0.0).astype(F32)
 
-    def smooth(src, dst, first, last):
+    def smooth(src, dst, first, last, skip=0):
         def get(t):
             if t < 0 or t > 59:
                 return [jnp.zeros((8, 128), F32)] * 2
@@ -432,18 +458,26 @@
             for h in range(2):
                 before = jnp.where(low, around[t - 2][h], around[t - 1][h])
                 after = jnp.where(low, around[t + 1][h], around[t + 2][h])
-                dst[t * 16 + 8 * h : t * 16 + 8 * h + 8, :] = here[h] + coef * (before + after - 2.0 * here[h])
+                dst[(t - skip) * 16 + 8 * h : (t - skip) * 16 + 8 * h + 8, :] = here[h] + coef * (before + after - 2.0 * here[h])
             del around[t - 2]
 
     smooth(full, tmp, 1, 58)
     smooth(tmp, full, 3, 56)
     smooth(full, tmp, 4, 55)
-    smooth(tmp, full, 6, 53)
+    smooth(tmp, moved, 6, 53, 6)
+    drain_x()
+    drain_sums()
+    drain_z()
+
+
+def relax_kernel(val, moved, phit, out, mac, mac_buf, coef_f, coef_l, keep, buf, out_sem, mac_sem):
     for t in range(TILES):
-        mac[:, t * 128 : (t + 1) * 128] = full[(t + 6) * 16 : (t + 6) * 16 + 13, :]
+        mac_buf[:, t * 128 : (t + 1) * 128] = moved[t * 16 : t * 16 + 13, :]
+    mac_copy = pltpu.make_async_copy(mac_buf, mac, mac_sem)
+    mac_copy.start()
 
     def row(k):
-        return jnp.tanh(full[pl.ds(96 + k, TILES, stride=16), :])
+        return jnp.tanh(moved[pl.ds(k, TILES, stride=16), :])
 
     density = 1.0 + 0.5 * row(0)
     ux, uy, uz = 0.5 * row(1), 0.5 * row(2), 0.5 * row(3)
@@ -484,8 +518,7 @@
 
     lhs_f = phit[:, 0:48].astype(BF16)
     lhs_l = phit[:, 48:96].astype(BF16)
-    keep = jnp.broadcast_to(phit[:, 96:97], (128, 128))
-    keep = jnp.concatenate([keep] * 3, axis=1)
+    keep[...] = jnp.broadcast_to(phit[:, 96:97], (128, 128))
 
     def split(ref, n):
         c = jnp.concatenate([ref[pl.ds(pl.multiple_of(n * 48 + 16 * j, 16), 16), :] for j in range(3)], axis=1)
@@ -493,47 +526,50 @@
         lo = (c - hi.astype(F32)).astype(BF16)
         return jnp.concatenate([hi, lo, hi], axis=0)
 
+    def put(n):
+        cols = pl.ds(pl.multiple_of(n * 384, 128), 384)
+        return pltpu.make_async_copy(buf.at[n % BUFS], out.at[:, :, cols], out_sem.at[n % BUFS])
+
     def relaxed(n, _):
-        cols = pl.ds(pl.multiple_of(n * 384, 128), 384)
+        @pl.when(n >= BUFS)
+        def _():
+            put(n - BUFS).wait()
+
         poly = jnp.dot(lhs_f, split(coef_f, n), preferred_element_type=F32)
         power = jnp.dot(lhs_l, split(coef_l, n), preferred_element_type=F32)
-        swept = val[:, :, cols].reshape(128, 384)
-        out[:, :, cols] = (keep * swept + poly * jnp.exp2(power)).reshape(2, 64, 384)
+        for j in range(3):
+            cols = pl.ds(pl.multiple_of(n * 384 + j * 128, 128), 128)
+            part = slice(j * 128, (j + 1) * 128)
+            swept = val[:, :, cols].reshape(128, 128)
+            buf[n % BUFS, :, :, part] = (keep[...] * swept + poly[:, part] * jnp.exp2(power[:, part])).reshape(2, 64, 128)
+        put(n).start()
         return 0
 
     lax.fori_loop(0, 16, relaxed, 0)
-
-    for g in range(GROUPS):
-        for t in range(1, NX):
-            @pl.when(gx + t < NX)
-            def _():
-                edge(0, t, g, (gx + t) % NX).wait_send()
-
-            @pl.when(gx - t >= 0)
-            def _():
-                edge(1, t, g, (gx - t) % NX).wait_send()
-
-    for n in range(4):
-        to_core(n).wait_send()
-    for n in range(3):
-        to_y(n).wait_send()
-    for n in range(7):
-        @pl.when((z + n + 1) % NZ < SLOT)
-        def _():
-            to_z(n).wait_send()
+    for n in range(16 - BUFS, 16):
+        put(n).wait()
+    mac_copy.wait()
 
 
 def per_device(dist, factors, velocity, weights, relax):
     vmem = pl.BlockSpec(memory_space=pltpu.VMEM)
-    return pl.pallas_call(
+    hbm = pl.BlockSpec(memory_space=pltpu.HBM)
+    operands = (dist, jnp.transpose(factors, (0, 2, 1)), velocity, weights, relax)
+    swept, moved, phit = pl.pallas_call(
         kernel,
         out_shape=(
             jax.ShapeDtypeStruct((2, 64, 6144), F32),
-            jax.ShapeDtypeStruct((13, 6144), F32),
+            jax.ShapeDtypeStruct((TILES * 16, 128), F32),
+            jax.ShapeDtypeStruct((128, 128), F32),
         ),
-        in_specs=[pl.BlockSpec(memory_space=pl.ANY), vmem, vmem, vmem, vmem],
-        out_specs=(vmem, vmem),
+        in_specs=[hbm] * 5,
+        out_specs=(vmem, vmem, vmem),
         scratch_shapes=[
+            pltpu.VMEM((2, 32, 64), F32),
+            pltpu.VMEM((3, 2, 64), F32),
+            pltpu.VMEM((13, 2, 64), F32),
+            pltpu.VMEM((2, 64), F32),
+            pltpu.VMEM((256, 128), BF16),
             pltpu.VMEM((2, 64, 6144), F32),
             pltpu.VMEM((2, 64, 6144), F32),
             pltpu.VMEM((2, 64, 256), F32),
@@ -541,9 +577,6 @@
             pltpu.VMEM((2, 64, 384), F32),
             pltpu.VMEM((32, 256), F32),
             pltpu.VMEM((128, 128), F32),
-            pltpu.VMEM((128, 128), F32),
-            pltpu.VMEM((TILES * 16, 128), F32),
-            pltpu.VMEM((TILES * 16, 128), F32),
             pltpu.VMEM((4 * SLOT_ROWS, 128), F32),
             pltpu.VMEM((4 * SLOT_ROWS, 128), F32),
             pltpu.VMEM((4 * SLOT_ROWS, 128), F32),
@@ -552,14 +585,33 @@
             pltpu.VMEM((10 * SLOT_ROWS, 128), F32),
             pltpu.VMEM((10 * SLOT_ROWS, 128), F32),
             pltpu.SemaphoreType.DMA((8,)),
-            pltpu.SemaphoreType.DMA((8,)),
+            pltpu.SemaphoreType.DMA((4,)),
             pltpu.SemaphoreType.DMA((N_SEM,)),
             pltpu.SemaphoreType.DMA((N_SEM,)),
         ],
         compiler_params=pltpu.CompilerParams(
-            collective_id=0, has_side_effects=True, vmem_limit_bytes=32 * 2**20
+            collective_id=0, has_side_effects=True, vmem_limit_bytes=40 * 2**20
         ),
-    )(dist, factors, velocity, weights, relax)
+    )(*[pltpu.with_memory_space_constraint(x, pltpu.HBM) for x in operands])
+    return pl.pallas_call(
+        relax_kernel,
+        out_shape=(
+            jax.ShapeDtypeStruct((2, 64, 6144), F32),
+            jax.ShapeDtypeStruct((13, 6144), F32),
+        ),
+        in_specs=[vmem] * 3,
+        out_specs=(hbm, hbm),
+        scratch_shapes=[
+            pltpu.VMEM((13, 6144), F32),
+            pltpu.VMEM((TILES * 16, 128), F32),
+            pltpu.VMEM((TILES * 16, 128), F32),
+            pltpu.VMEM((128, 128), F32),
+            pltpu.VMEM((BUFS, 2, 64, 384), F32),
+            pltpu.SemaphoreType.DMA((BUFS,)),
+            pltpu.SemaphoreType.DMA,
+        ],
+        compiler_params=pltpu.CompilerParams(vmem_limit_bytes=32 * 2**20),
+    )(swept, moved, phit)
 
 
 def solution(mesh):

time: 61.3 us -> 49 us (0.80)
  local copies, waits for them, and re-layouts: 7.21 us -> 0 us
  Pallas kernels: 53.2 us -> 48.2 us
    pallas_call x1, Pallas kernels: 53.2 us -> 43.2 us  [per_device(): pl.pallas_call(kernel, out_shape=(jax.ShapeDtypeStruct((2, 64, 6144), F32...]
    unnamed x11 -> x0, local copies, waits for them, and re-layouts: 7.21 us -> none
    pallas_call x0 -> x1, Pallas kernels: none -> 5.03 us  [per_device(): pl.pallas_call(relax_kernel, out_shape=(jax.ShapeDtypeStruct((2, 64, 6144...]
where the time goes in v2:
time: 49 us; the launch traced here: 48.9 us
  Pallas kernels  48.2 us (98%)
  between operations  0.64 us (1%)
    pallas_call x1, Pallas kernels, per_device(): pl.pallas_call(kernel, out_shape=(jax.ShapeDtypeStruct((2, 64, 6144), F32...  43.2 us
    pallas_call x1, Pallas kernels, per_device(): pl.pallas_call(relax_kernel, out_shape=(jax.ShapeDtypeStruct((2, 64, 6144...  5.03 us

profile of v2, /device:TPU:1, one launch (start us, length us, event | category | flops | bytes accessed | tf_op | source)
XLA Modules:
  0.0 48.9 jit_solution(14104398644834402501)
XLA Ops:
  0.6 43.2 %shard_map.68 = (f32[2,64,6144]{2,1,0:T(8,128)S(1)}, f32[768,128]{1,0:T(8,128)S(1)}, f32[128,128]{1,0:T(8,128)S(1)}) custom-call(f32[2,64,6144]{2,1,0:T(8,128)} %dist.1, f32[2,32,64]{2,1,0:T(8,128)} %bitcast.1, f32[3,2,64]{2,1,0:T(2,128)} %vel_hbm.1, f32[13,2,64]{2,1,0:T(2,128)} %wgt_hbm.1, f32[2,64]{1,0:T(2,128)} %rel_hbm.1), custom_call_target="tpu_custom_call" | custom-call | tf_op jit(solution)/shard_map/pallas_call | solution.py:558
  43.9 5.0 %shard_map.69 = (f32[2,64,6144]{2,1,0:T(8,128)}, f32[13,6144]{1,0:T(8,128)}) custom-call(f32[2,64,6144]{2,1,0:T(8,128)S(1)} %get-tuple-element.5.val, f32[768,128]{1,0:T(8,128)S(1)} %get-tuple-element.6.moved, f32[128,128]{1,0:T(8,128)S(1)} %get-tuple-element.7.phit), custom_call_target="tpu_custom_call" | custom-call | tf_op jit(solution)/shard_map/pallas_call | solution.py:596

commit v3 on v2

--- a/solution.py
+++ b/solution.py
@@ -30,7 +30,7 @@
 
 def kernel(
     dist, fac_hbm, vel_hbm, wgt_hbm, rel_hbm, val, moved, phit,
-    fac, vel, wgt, rel, lhs, reach, scaled, snd, rcv, inc, wmat, phi,
+    fac, vel, wgt, rel, lhs, reach, scaled, spread_f, snd, rcv, inc, wmat, phi,
     stage, part, got_c, got_y, got_z, full, tmp, ld_sem, small_sem, ssem, rsem,
 ):
     gx = lax.axis_index("gx")
@@ -93,24 +93,134 @@
         return jnp.concatenate([a, b], axis=1)
 
     small[0].wait()
-    compact = lanes2(fac[0], fac[1])
-    for n, x in enumerate((compact, jnp.sqrt(1.0 - compact * compact))):
+    f = lanes2(fac[0], fac[1])
+    q = jnp.sqrt(1.0 - f * f)
+    at = lax.broadcasted_iota(jnp.int32, (32, 128), 0)
+    ahead = lax.broadcasted_iota(jnp.int32, (32, 128), 1) < 64
+
+    def down(x, k):
+        return jnp.where(at >= k, pltpu.roll(x, k, 0), 1.0)
+
+    def up(x, k):
+        return jnp.where(at < 32 - k, pltpu.roll(x, 32 - k, 0), 1.0)
+
+    before, after = f, f
+    for k in (1, 2, 4, 8, 16):
+        before, after = before * down(before, k), after * up(after, k)
+    to_edge = q * jnp.where(ahead, up(after, 1), down(before, 1))
+
+    def exact(x, n, extra):
         hi = x.astype(BF16).astype(F32)
         mid = (x - hi).astype(BF16).astype(F32)
-        parts = jnp.concatenate([hi, mid, x - hi - mid, jnp.zeros_like(x)], axis=0)
-        lhs[n * 128 : (n + 1) * 128, :] = parts.T.astype(BF16)
-
-    def spread(p, _):
+        turned = jnp.concatenate([hi, mid, x - hi - mid, extra], axis=0).T
+        lhs[n * 128 : (n + 1) * 128, :] = turned.astype(BF16)
+        return turned
+
+    def picks(p):
         cell = lax.broadcasted_iota(jnp.int32, (96, 384), 0) % 32
         second = lax.broadcasted_iota(jnp.int32, (96, 384), 1) >= 192
-        picks = jnp.where(cell == 2 * p + jnp.where(second, 1, 0), 1.0, 0.0).astype(BF16)
-        cols = pl.ds(pl.multiple_of(p * 384, 128), 384)
-        both = jnp.dot(lhs[:, 0:96], picks, preferred_element_type=F32)
-        reach[:, :, cols] = both[0:128].reshape(2, 64, 384)
-        scaled[:, :, cols] = both[128:256].reshape(2, 64, 384)
-        return 0
-
-    lax.fori_loop(0, 16, spread, 0)
+        return jnp.where(cell == 2 * p + jnp.where(second, 1, 0), 1.0, 0.0).astype(BF16)
+
+    def spread(first, refs, unroll):
+        def some(n, _):
+            for k in range(unroll):
+                p = n * unroll + k
+                cols = pl.ds(pl.multiple_of(p * 384, 128), 384)
+                rows = lhs[first * 128 : (first + len(refs)) * 128, 0:96]
+                wide = jnp.dot(rows, picks(p), preferred_element_type=F32)
+                for m, ref in enumerate(refs):
+                    ref[:, :, cols] = wide[m * 128 : (m + 1) * 128].reshape(2, 64, 384)
+            return 0
+
+        lax.fori_loop(0, 16 // unroll, some, 0)
+
+    phi[...] = exact(to_edge, 0, after)
+    spread(0, [scaled], 4)
+
+    def leave(r):
+        rows = rows8(r)
+        for d in range(2):
+            total = [None] * 3
+            for t in range(TILES):
+                term = scaled[d, rows, t * 128 : (t + 1) * 128] * val[d, rows, t * 128 : (t + 1) * 128]
+                total[t % 3] = term if total[t % 3] is None else total[t % 3] + term
+            a, b, c = total
+            through = jnp.broadcast_to(phi[pl.ds(pl.multiple_of(d * 64 + r * 8, 8), 8), 96:97], (8, 128))
+            if d == 0:
+                ra, rb = pltpu.roll(a, 64, 1), pltpu.roll(b, 64, 1)
+                snd[0, rows, 0:128] = jnp.where(low, through, b + ra)
+                snd[0, rows, 128:256] = c + jnp.where(low, ra, rb)
+            else:
+                rb, rc = pltpu.roll(b, 64, 1), pltpu.roll(c, 64, 1)
+                snd[1, rows, 0:128] = a + jnp.where(low, rb, rc)
+                snd[1, rows, 128:256] = jnp.where(low, b + rc, through)
+
+    def edge(direction, t, g, target):
+        span = pl.ds(g * (64 // GROUPS), 64 // GROUPS)
+        n = XF + (direction * 3 + t - 1) * GROUPS + g
+        return copy(snd.at[direction, span, :], rcv.at[direction, t - 1, span, :], n, n, target, vert)
+
+    def drain_x():
+        for g in range(GROUPS):
+            for t in range(1, NX):
+                @pl.when(gx + t < NX)
+                def _():
+                    edge(0, t, g, (gx + t) % NX).wait_send()
+
+                @pl.when(gx - t >= 0)
+                def _():
+                    edge(1, t, g, (gx - t) % NX).wait_send()
+
+    for g in range(GROUPS):
+        def leave_rows(r, _):
+            load(r).wait()
+            leave(r)
+            return 0
+
+        lax.fori_loop(g * 8 // GROUPS, (g + 1) * 8 // GROUPS, leave_rows, 0)
+        if g == 0:
+            pl.semaphore_wait(barrier, 14 + jnp.where(halo_source, 3, 0))
+
+        for t in (2, 1, 3):
+            @pl.when(gx + t < NX)
+            def _():
+                edge(0, t, g, gx + t).start()
+
+            @pl.when(gx - t >= 0)
+            def _():
+                edge(1, t, g, gx - t).start()
+
+    for one_copy in small[1:]:
+        one_copy.wait()
+    wmat[...] = jnp.zeros_like(wmat)
+    for k in range(13):
+        row = lanes2(wgt[k, 0:1, :], wgt[k, 1:2, :])
+        hi = row.astype(BF16).astype(F32)
+        lo = row - hi
+        wmat[k : k + 1, 0:128] = hi
+        wmat[k : k + 1, 128:256] = hi
+        wmat[16 + k : 17 + k, 0:128] = lo
+
+    vx, vy, vz = [lanes2(vel[j, 0:1, :], vel[j, 1:2, :]) for j in range(3)]
+    relax = lanes2(rel[0:1, :], rel[1:2, :])
+    xx, yy, zz = vx * vx, vy * vy, vz * vz
+    sq = xx + yy + zz
+    one = jnp.ones_like(vx)
+    feats = [vx * sq, vy * sq, vz * sq, xx, yy, zz, vx * vy, vx * vz, vy * vz, vx, vy, vz, one]
+    phi[...] = jnp.zeros_like(phi)
+    for n, feat in enumerate(feats):
+        for base, term in ((0, feat * relax), (48, feat)):
+            hi = term.astype(BF16).astype(F32)
+            phi[base + n : base + n + 1, :] = hi
+            phi[base + 16 + n : base + 17 + n, :] = hi
+            phi[base + 32 + n : base + 33 + n, :] = term - hi
+    phi[96:97, :] = 1.0 - relax
+    phit[...] = phi[...].T
+
+    exact(f, 1, f)
+    exact(q, 2, q)
+    exact(jnp.where(ahead, before, after), 3, f)
+    spread(1, [spread_f, scaled, reach], 2)
 
     def sweep(r):
         rows = rows8(r)
@@ -121,13 +231,12 @@
             return pl.ds(t * 128, 128)
 
         value = [[zero] * 3, [zero] * 3]
-        total = [[ones] * 3, [ones] * 3]
         rolls = [[zero, zero], [zero, zero]]
         f_near = [ones, ones]
         for step in range(16):
             for d in range(2):
                 p = step if d == 0 else 15 - step
-                f = [reach[d, rows, cols(3 * p + j)] for j in range(3)]
+                f = [spread_f[d, rows, cols(3 * p + j)] for j in range(3)]
                 first, second = (f[0], f[2]) if d == 0 else (f[2], f[0])
                 near, far = first * f_near[d], second * first
                 f_near[d] = second
@@ -142,75 +251,13 @@
                     neighbour = jnp.where(low, two_off, one_off) if d == 0 else jnp.where(low, one_off, two_off)
                     rolls[d] = [one_off, pltpu.roll(s, 64, 1)]
                     value[d][j] = gs[j] * value[d][j] + (s + f[j] * neighbour)
-                    total[d][j] = gs[j] * total[d][j]
                     val[d, rows, cols(t)] = value[d][j]
-                    reach[d, rows, cols(t)] = total[d][j]
-        snd[0, rows, 0:128] = jnp.where(low, total[0][2], value[0][1])
-        snd[0, rows, 128:256] = value[0][2]
-        snd[1, rows, 0:128] = value[1][0]
-        snd[1, rows, 128:256] = jnp.where(low, value[1][1], total[1][0])
-
-    def edge(direction, t, g, target):
-        span = pl.ds(g * (64 // GROUPS), 64 // GROUPS)
-        n = XF + (direction * 3 + t - 1) * GROUPS + g
-        return copy(snd.at[direction, span, :], rcv.at[direction, t - 1, span, :], n, n, target, vert)
-
-    def drain_x():
-        for g in range(GROUPS):
-            for t in range(1, NX):
-                @pl.when(gx + t < NX)
-                def _():
-                    edge(0, t, g, (gx + t) % NX).wait_send()
-
-                @pl.when(gx - t >= 0)
-                def _():
-                    edge(1, t, g, (gx - t) % NX).wait_send()
-
-    for g in range(GROUPS):
-        def sweep_rows(r, _):
-            load(r).wait()
-            sweep(r)
-            return 0
-
-        lax.fori_loop(g * 8 // GROUPS, (g + 1) * 8 // GROUPS, sweep_rows, 0)
-        if g == 0:
-            pl.semaphore_wait(barrier, 14 + jnp.where(halo_source, 3, 0))
-
-        for t in range(1, NX):
-            @pl.when(gx + t < NX)
-            def _():
-                edge(0, t, g, gx + t).start()
-
-            @pl.when(gx - t >= 0)
-            def _():
-                edge(1, t, g, gx - t).start()
-
-    for one_copy in small[1:]:
-        one_copy.wait()
-    wmat[...] = jnp.zeros_like(wmat)
-    for k in range(13):
-        row = lanes2(wgt[k, 0:1, :], wgt[k, 1:2, :])
-        hi = row.astype(BF16).astype(F32)
-        lo = row - hi
-        wmat[k : k + 1, 0:128] = hi
-        wmat[k : k + 1, 128:256] = hi
-        wmat[16 + k : 17 + k, 0:128] = lo
-
-    vx, vy, vz = [lanes2(vel[j, 0:1, :], vel[j, 1:2, :]) for j in range(3)]
-    relax = lanes2(rel[0:1, :], rel[1:2, :])
-    xx, yy, zz = vx * vx, vy * vy, vz * vz
-    sq = xx + yy + zz
-    one = jnp.ones_like(vx)
-    feats = [vx * sq, vy * sq, vz * sq, xx, yy, zz, vx * vy, vx * vz, vy * vz, vx, vy, vz, one]
-    phi[...] = jnp.zeros_like(phi)
-    for n, feat in enumerate(feats):
-        for base, f in ((0, feat * relax), (48, feat)):
-            hi = f.astype(BF16).astype(F32)
-            phi[base + n : base + n + 1, :] = hi
-            phi[base + 16 + n : base + 17 + n, :] = hi
-            phi[base + 32 + n : base + 33 + n, :] = f - hi
-    phi[96:97, :] = 1.0 - relax
-    phit[...] = phi[...].T
+
+    def sweep_rows(r, _):
+        sweep(r)
+        return 0
+
+    lax.fori_loop(0, 8, sweep_rows, 0)
 
     for t in range(1, NX):
         for g in range(GROUPS):
@@ -334,7 +381,8 @@
             def _():
                 to_z(n).wait_send()
 
-    for n in range(7):
+    far_first = (3, 2, 4, 1, 5, 0, 6)
+    for n in far_first:
         @pl.when((z + n + 1) % NZ < SLOT)
         def _():
             to_z(n).start()
@@ -346,7 +394,7 @@
             copy(got_z.at[tile_rows(n), :], got_z.at[tile_rows(n), :], ZR + n, ZR + n, gx, vert).wait_recv()
             total += got_z[tile_rows(n), :]
         full[pl.ds(pl.multiple_of(own_row + z * 16, 16), 16), :] = total
-        for n in range(7):
+        for n in far_first:
             from_owner(n, z, (z + n + 1) % NZ).start()
 
     for n in range(7):
@@ -375,16 +423,16 @@
     def gather_core(n, slot):
         return copy(full.at[slot_of(slot), :], full.at[slot_of(slot), :], CG + n, CG + n, gx, partner)
 
-    for n in range(3):
+    @pl.when(halo_source)
+    def _():
+        for n in (2, 1, 3, 0):
+            send_halo(n).start()
+
+    for n in (1, 0, 2):
         gather_y(n, mine).start()
 
-    @pl.when(halo_source)
-    def _():
-        for n in range(4):
-            send_halo(n).start()
-
     gather_core(3, mine).start()
-    for n in range(3):
+    for n in (0, 2, 1):
         slot = core * 4 + (y + NY - n - 1) % NY
         gather_y(n, slot).wait_recv()
         gather_core(n, slot).start()
@@ -545,7 +593,12 @@
         put(n).start()
         return 0
 
-    lax.fori_loop(0, 16, relaxed, 0)
+    def two(n, _):
+        relaxed(2 * n, 0)
+        relaxed(2 * n + 1, 0)
+        return 0
+
+    lax.fori_loop(0, 8, two, 0)
     for n in range(16 - BUFS, 16):
         put(n).wait()
     mac_copy.wait()
@@ -569,7 +622,8 @@
             pltpu.VMEM((3, 2, 64), F32),
             pltpu.VMEM((13, 2, 64), F32),
             pltpu.VMEM((2, 64), F32),
-            pltpu.VMEM((256, 128), BF16),
+            pltpu.VMEM((512, 128), BF16),
+            pltpu.VMEM((2, 64, 6144), F32),
             pltpu.VMEM((2, 64, 6144), F32),
             pltpu.VMEM((2, 64, 6144), F32),
             pltpu.VMEM((2, 64, 256), F32),

time: 49 us -> 46.7 us (0.953)
  Pallas kernels: 48.2 us -> 46 us
    pallas_call x1, Pallas kernels: 43.2 us -> 41.1 us  [per_device(): pl.pallas_call(kernel, out_shape=(jax.ShapeDtypeStruct((2, 64, 6144), F32...]
where the time goes in v3:
time: 46.7 us; the launch traced here: 46.6 us
  Pallas kernels  46 us (99%)
  between operations  0.64 us (1%)
    pallas_call x1, Pallas kernels, per_device(): pl.pallas_call(kernel, out_shape=(jax.ShapeDtypeStruct((2, 64, 6144), F32...  41.1 us
    pallas_call x1, Pallas kernels, per_device(): pl.pallas_call(relax_kernel, out_shape=(jax.ShapeDtypeStruct((2, 64, 6144...  4.88 us

profile of v3, /device:TPU:1, one launch (start us, length us, event | category | flops | bytes accessed | tf_op | source)
XLA Modules:
  0.0 46.6 jit_solution(6447114289333151139)
XLA Ops:
  0.6 41.1 %shard_map.68 = (f32[2,64,6144]{2,1,0:T(8,128)S(1)}, f32[768,128]{1,0:T(8,128)S(1)}, f32[128,128]{1,0:T(8,128)S(1)}) custom-call(f32[2,64,6144]{2,1,0:T(8,128)} %dist.1, f32[2,32,64]{2,1,0:T(8,128)} %bitcast.1, f32[3,2,64]{2,1,0:T(2,128)} %vel_hbm.1, f32[13,2,64]{2,1,0:T(2,128)} %wgt_hbm.1, f32[2,64]{1,0:T(2,128)} %rel_hbm.1), custom_call_target="tpu_custom_call" | custom-call | tf_op jit(solution)/shard_map/pallas_call | solution.py:611
  41.7 4.9 %shard_map.69 = (f32[2,64,6144]{2,1,0:T(8,128)}, f32[13,6144]{1,0:T(8,128)}) custom-call(f32[2,64,6144]{2,1,0:T(8,128)S(1)} %get-tuple-element.5.val, f32[768,128]{1,0:T(8,128)S(1)} %get-tuple-element.6.moved, f32[128,128]{1,0:T(8,128)S(1)} %get-tuple-element.7.phit), custom_call_target="tpu_custom_call" | custom-call | tf_op jit(solution)/shard_map/pallas_call | solution.py:650

commit v4 on v3

--- a/solution.py
+++ b/solution.py
@@ -14,11 +14,10 @@
 
 NX, NY, NZ = 4, 4, 8
 TILES, SLOT = 48, 6
-SLOT_ROWS = SLOT * 16
-GROUPS = 2
-BUFS = 4
-
-XF, CR = 0, 6 * GROUPS
+SLOT_ROWS, OWNERS = 80, 5
+AWAY = (2, 1, 3, 0)
+
+XF, CR = 0, 6
 YR = CR + 4
 ZR = YR + 3
 ZG = ZR + 7
@@ -30,8 +29,8 @@
 
 def kernel(
     dist, fac_hbm, vel_hbm, wgt_hbm, rel_hbm, val, moved, phit,
-    fac, vel, wgt, rel, lhs, reach, scaled, spread_f, snd, rcv, inc, wmat, phi,
-    stage, part, got_c, got_y, got_z, full, tmp, ld_sem, small_sem, ssem, rsem,
+    fac, vel, wgt, rel, picks, lhs, reach, scaled, spread_f, snd, rcv, inc, wmat, phi,
+    stage, part, got_c, got_y, got_z, full, tmp, again, ld_sem, small_sem, ssem, rsem,
 ):
     gx = lax.axis_index("gx")
     vert = lax.axis_index("vert")
@@ -51,8 +50,9 @@
     def rows8(r):
         return pl.ds(pl.multiple_of(r * 8, 8), 8)
 
-    def load(r):
-        return pltpu.make_async_copy(dist.at[:, rows8(r), :], val.at[:, rows8(r), :], ld_sem.at[r])
+    def load(n):
+        d, cols = n // 4, pl.ds(n % 4 * 1536, 1536)
+        return pltpu.make_async_copy(dist.at[d, :, cols], val.at[d, :, cols], ld_sem.at[n])
 
     small = [
         pltpu.make_async_copy(src, dst, small_sem.at[n])
@@ -92,6 +92,11 @@
     def lanes2(a, b):
         return jnp.concatenate([a, b], axis=1)
 
+    cell = lax.broadcasted_iota(jnp.int32, (96, 384), 0) % 32
+    cell -= jnp.where(lax.broadcasted_iota(jnp.int32, (96, 384), 1) >= 192, 1, 0)
+    for p in range(16):
+        picks[:, p * 384 : (p + 1) * 384] = jnp.where(cell == 2 * p, 1.0, 0.0).astype(BF16)
+
     small[0].wait()
     f = lanes2(fac[0], fac[1])
     q = jnp.sqrt(1.0 - f * f)
@@ -116,18 +121,13 @@
         lhs[n * 128 : (n + 1) * 128, :] = turned.astype(BF16)
         return turned
 
-    def picks(p):
-        cell = lax.broadcasted_iota(jnp.int32, (96, 384), 0) % 32
-        second = lax.broadcasted_iota(jnp.int32, (96, 384), 1) >= 192
-        return jnp.where(cell == 2 * p + jnp.where(second, 1, 0), 1.0, 0.0).astype(BF16)
-
     def spread(first, refs, unroll):
         def some(n, _):
             for k in range(unroll):
                 p = n * unroll + k
                 cols = pl.ds(pl.multiple_of(p * 384, 128), 384)
                 rows = lhs[first * 128 : (first + len(refs)) * 128, 0:96]
-                wide = jnp.dot(rows, picks(p), preferred_element_type=F32)
+                wide = jnp.dot(rows, picks[:, cols], preferred_element_type=F32)
                 for m, ref in enumerate(refs):
                     ref[:, :, cols] = wide[m * 128 : (m + 1) * 128].reshape(2, 64, 384)
             return 0
@@ -135,63 +135,79 @@
         lax.fori_loop(0, 16 // unroll, some, 0)
 
     phi[...] = exact(to_edge, 0, after)
-    spread(0, [scaled], 4)
-
-    def leave(r):
-        rows = rows8(r)
-        for d in range(2):
-            total = [None] * 3
-            for t in range(TILES):
-                term = scaled[d, rows, t * 128 : (t + 1) * 128] * val[d, rows, t * 128 : (t + 1) * 128]
-                total[t % 3] = term if total[t % 3] is None else total[t % 3] + term
-            a, b, c = total
-            through = jnp.broadcast_to(phi[pl.ds(pl.multiple_of(d * 64 + r * 8, 8), 8), 96:97], (8, 128))
+
+    for d in range(2):
+        through = jnp.zeros((8, 128), F32)
+        for r in range(8):
+            through = jnp.where(lane == r, phi[d * 64 + r * 8 : d * 64 + r * 8 + 8, 96:97], through)
+        snd[d, 0:8, :] = through
+
+    def whole_row(r):
+        return 8 + 8 * r
+
+    def half_row(pair):
+        return 72 + 8 * pair
+
+    def leave(d):
+        total = None
+        for p in range(16):
+            if p % 4 == 0:
+                load(d * 4 + p // 4).wait()
+            cols = slice(p * 384, (p + 1) * 384)
+            weight = jnp.dot(lhs[d * 64 : d * 64 + 64, 0:96], picks[:, cols], preferred_element_type=F32)
+            term = weight * val[d, :, cols]
+            total = term if total is None else total + term
+        halves = []
+        for r in range(8):
+            a, b, c = [total[8 * r : 8 * r + 8, j * 128 : (j + 1) * 128] for j in range(3)]
+            rb = pltpu.roll(b, 64, 1)
             if d == 0:
-                ra, rb = pltpu.roll(a, 64, 1), pltpu.roll(b, 64, 1)
-                snd[0, rows, 0:128] = jnp.where(low, through, b + ra)
-                snd[0, rows, 128:256] = c + jnp.where(low, ra, rb)
+                ra = pltpu.roll(a, 64, 1)
+                snd[d, whole_row(r) : whole_row(r) + 8, :] = c + jnp.where(low, ra, rb)
+                halves.append(b + ra)
             else:
-                rb, rc = pltpu.roll(b, 64, 1), pltpu.roll(c, 64, 1)
-                snd[1, rows, 0:128] = a + jnp.where(low, rb, rc)
-                snd[1, rows, 128:256] = jnp.where(low, b + rc, through)
-
-    def edge(direction, t, g, target):
-        span = pl.ds(g * (64 // GROUPS), 64 // GROUPS)
-        n = XF + (direction * 3 + t - 1) * GROUPS + g
-        return copy(snd.at[direction, span, :], rcv.at[direction, t - 1, span, :], n, n, target, vert)
+                rc = pltpu.roll(c, 64, 1)
+                snd[d, whole_row(r) : whole_row(r) + 8, :] = a + jnp.where(low, rb, rc)
+                halves.append(b + rc)
+        for pair in range(4):
+            one, other = halves[pair], halves[pair + 4]
+            if d == 0:
+                both = jnp.where(low, pltpu.roll(one, 64, 1), other)
+            else:
+                both = jnp.where(low, one, pltpu.roll(other, 64, 1))
+            snd[d, half_row(pair) : half_row(pair) + 8, :] = both
+
+    def edge(direction, t, target):
+        n = XF + direction * 3 + t - 1
+        return copy(snd.at[direction], rcv.at[direction, t - 1], n, n, target, vert)
 
     def drain_x():
-        for g in range(GROUPS):
-            for t in range(1, NX):
-                @pl.when(gx + t < NX)
-                def _():
-                    edge(0, t, g, (gx + t) % NX).wait_send()
-
-                @pl.when(gx - t >= 0)
-                def _():
-                    edge(1, t, g, (gx - t) % NX).wait_send()
-
-    for g in range(GROUPS):
-        def leave_rows(r, _):
-            load(r).wait()
-            leave(r)
-            return 0
-
-        lax.fori_loop(g * 8 // GROUPS, (g + 1) * 8 // GROUPS, leave_rows, 0)
-        if g == 0:
-            pl.semaphore_wait(barrier, 14 + jnp.where(halo_source, 3, 0))
-
-        for t in (2, 1, 3):
+        for t in range(1, NX):
             @pl.when(gx + t < NX)
             def _():
-                edge(0, t, g, gx + t).start()
+                edge(0, t, (gx + t) % NX).wait_send()
 
             @pl.when(gx - t >= 0)
             def _():
-                edge(1, t, g, gx - t).start()
+                edge(1, t, (gx - t) % NX).wait_send()
+
+    for d in range(2):
+        leave(d)
+        if d == 0:
+            pl.semaphore_wait(barrier, 14 + jnp.where(halo_source, 3, 0))
+        for t in (2, 1, 3):
+            target = gx + t if d == 0 else gx - t
+
+            @pl.when((target >= 0) & (target < NX))
+            def _():
+                edge(d, t, target).start()
 
     for one_copy in small[1:]:
         one_copy.wait()
+    for n in range(4):
+        for ref in (stage, part):
+            ref[n * SLOT_ROWS + 72 : n * SLOT_ROWS + 80, :] = jnp.zeros((8, 128), F32)
+    full[10 * SLOT_ROWS : 10 * SLOT_ROWS + 8, :] = jnp.zeros((8, 128), F32)
     wmat[...] = jnp.zeros_like(wmat)
     for k in range(13):
         row = lanes2(wgt[k, 0:1, :], wgt[k, 1:2, :])
@@ -260,46 +276,45 @@
     lax.fori_loop(0, 8, sweep_rows, 0)
 
     for t in range(1, NX):
-        for g in range(GROUPS):
-            @pl.when(gx - t >= 0)
-            def _():
-                edge(0, t, g, (gx - t) % NX).wait_recv()
-
-            @pl.when(gx + t < NX)
-            def _():
-                edge(1, t, g, (gx + t) % NX).wait_recv()
-
-    def enter(r, _):
-        rows = rows8(r)
-        zero = jnp.zeros((8, 128), F32)
-
-        def forward(n, state):
-            a, b = state
-            ra, rb = rcv[0, gx - n - 1, rows, 0:128], rcv[0, gx - n - 1, rows, 128:256]
-            through = jnp.broadcast_to(ra[:, 0:1], (8, 128))
-            return through * a + ra, through * b + rb
-
-        a, b = lax.fori_loop(0, gx, forward, (zero, zero))
-        ra, rb = pltpu.roll(a, 64, 1), pltpu.roll(b, 64, 1)
-        inc[0, rows, 0:128] = jnp.where(low, ra, rb)
-        inc[0, rows, 128:256] = jnp.where(low, rb, a)
-        inc[0, rows, 256:384] = b
-
-        def backward(n, state):
-            a, b = state
-            last = NX - 2 - gx - n
-            ra, rb = rcv[1, last, rows, 0:128], rcv[1, last, rows, 128:256]
-            through = jnp.broadcast_to(rb[:, 127:128], (8, 128))
-            return through * a + ra, through * b + rb
-
-        a, b = lax.fori_loop(0, NX - 1 - gx, backward, (zero, zero))
-        ra, rb = pltpu.roll(a, 64, 1), pltpu.roll(b, 64, 1)
-        inc[1, rows, 0:128] = a
-        inc[1, rows, 128:256] = jnp.where(low, b, ra)
-        inc[1, rows, 256:384] = jnp.where(low, ra, rb)
-        return 0
-
-    lax.fori_loop(0, 8, enter, 0)
+        @pl.when(gx - t >= 0)
+        def _():
+            edge(0, t, (gx - t) % NX).wait_recv()
+
+        @pl.when(gx + t < NX)
+        def _():
+            edge(1, t, (gx + t) % NX).wait_recv()
+
+    def entering(d):
+        def add(n, state):
+            slot = gx - n - 1 if d == 0 else NX - 2 - gx - n
+            products = rcv[d, slot, 0:8, :]
+            through = [jnp.broadcast_to(products[:, r : r + 1], (8, 128)) for r in range(8)]
+            new = []
+            for r in range(8):
+                new.append(through[r] * state[r] + rcv[d, slot, whole_row(r) : whole_row(r) + 8, :])
+            for pair in range(4):
+                mixed = jnp.where(low, through[pair], through[pair + 4])
+                new.append(mixed * state[8 + pair] + rcv[d, slot, half_row(pair) : half_row(pair) + 8, :])
+            return tuple(new)
+
+        state = lax.fori_loop(0, gx if d == 0 else NX - 1 - gx, add, (jnp.zeros((8, 128), F32),) * 12)
+        for pair in range(4):
+            h = state[8 + pair]
+            turned = pltpu.roll(h, 64, 1)
+            for k in range(2):
+                r = pair + 4 * k
+                a = state[r]
+                ra = pltpu.roll(a, 64, 1)
+                at_low, at_high = (h, turned) if k == 0 else (turned, h)
+                if d == 0:
+                    tiles = (jnp.where(low, at_low, ra), jnp.where(low, ra, at_high), a)
+                else:
+                    tiles = (a, jnp.where(low, at_low, ra), jnp.where(low, ra, at_high))
+                for j in range(3):
+                    inc[d, 8 * r : 8 * r + 8, j * 128 : (j + 1) * 128] = tiles[j]
+
+    entering(0)
+    entering(1)
 
     weights = wmat[...].astype(BF16)
 
@@ -314,10 +329,10 @@
             both = jnp.dot(weights, jnp.concatenate([hi, lo], axis=0), preferred_element_type=F32)
             total = both[0:16] + both[16:32]
             for j in range(3):
-                dst[pl.ds(pl.multiple_of(dst_row + (half * 3 + j) * 16, 16), 16), :] = total[:, j * 128 : (j + 1) * 128]
+                dst[pl.ds(dst_row + (half * 3 + j) * 13, 13), :] = total[0:13, j * 128 : (j + 1) * 128]
 
     def slot_rows(n):
-        return pl.ds(pl.multiple_of(n * SLOT_ROWS, SLOT_ROWS), SLOT_ROWS)
+        return pl.ds(n * SLOT_ROWS, SLOT_ROWS)
 
     partner = vert_of(y, z, 1 - core)
 
@@ -325,29 +340,28 @@
         return copy(stage.at[slot_rows(n), :], got_c.at[slot_rows(n), :], CR + n, CR + n, gx, partner)
 
     def other_half(n, _):
-        moments((1 - core) * 4 + (y + n + 1) % NY, stage, n * SLOT_ROWS)
+        moments((1 - core) * 4 + (y + AWAY[n]) % NY, stage, n * SLOT_ROWS)
         to_core(n).start()
         return 0
 
-    lax.fori_loop(0, 4, other_half, 0)
+    for n in range(4):
+        other_half(n, 0)
 
     def to_y(n):
         return copy(
-            part.at[slot_rows(n), :], got_y.at[slot_rows(n), :], YR + n, YR + n, gx, vert_of((y + n + 1) % NY, z, core)
+            part.at[slot_rows(n), :], got_y.at[slot_rows(n), :], YR + n, YR + n, gx, vert_of((y + AWAY[n]) % NY, z, core)
         )
 
     def own_half(n, _):
-        moments(core * 4 + (y + n + 1) % NY, part, n * SLOT_ROWS)
+        moments(core * 4 + (y + AWAY[n]) % NY, part, n * SLOT_ROWS)
         to_core(n).wait_recv()
         part[slot_rows(n), :] += got_c[slot_rows(n), :]
 
-        @pl.when(n < 3)
-        def _():
+        if n < 3:
             to_y(n).start()
 
-        return 0
-
-    lax.fori_loop(0, 4, own_half, 0)
+    for n in range(4):
+        own_half(n, 0)
     for n in range(3):
         to_y(n).wait_recv()
         part[slot_rows(3), :] += got_y[slot_rows(n), :]
@@ -377,17 +391,17 @@
 
     def drain_z():
         for n in range(7):
-            @pl.when((z + n + 1) % NZ < SLOT)
+            @pl.when((z + n + 1) % NZ < OWNERS)
             def _():
                 to_z(n).wait_send()
 
     far_first = (3, 2, 4, 1, 5, 0, 6)
     for n in far_first:
-        @pl.when((z + n + 1) % NZ < SLOT)
+        @pl.when((z + n + 1) % NZ < OWNERS)
         def _():
             to_z(n).start()
 
-    @pl.when(z < SLOT)
+    @pl.when(z < OWNERS)
     def _():
         total = part[pl.ds(pl.multiple_of(3 * SLOT_ROWS + z * 16, 16), 16), :]
         for n in range(7):
@@ -400,7 +414,7 @@
     for n in range(7):
         owner = (z + NZ - n - 1) % NZ
 
-        @pl.when(owner < SLOT)
+        @pl.when(owner < OWNERS)
         def _():
             from_owner(n, owner, z).wait_recv()
 
@@ -476,7 +490,7 @@
     def _():
         gather_core(4, halo_slot).wait_send()
 
-    @pl.when(z < SLOT)
+    @pl.when(z < OWNERS)
     def _():
         for n in range(7):
             from_owner(n, z, (z + n + 1) % NZ).wait_send()
@@ -488,7 +502,8 @@
         def get(t):
             if t < 0 or t > 59:
                 return [jnp.zeros((8, 128), F32)] * 2
-            return [src[t * 16 + 8 * h : t * 16 + 8 * h + 8, :] for h in range(2)]
+            row = t // SLOT * SLOT_ROWS + t % SLOT * 13 if src is full else t * 16
+            return [src[row + 8 * h : row + 8 * h + 8, :] for h in range(2)]
 
         def rolled(t):
             return [pltpu.roll(m, 64, 1) for m in get(t)]
@@ -510,8 +525,8 @@
             del around[t - 2]
 
     smooth(full, tmp, 1, 58)
-    smooth(tmp, full, 3, 56)
-    smooth(full, tmp, 4, 55)
+    smooth(tmp, again, 3, 56)
+    smooth(again, tmp, 4, 55)
     smooth(tmp, moved, 6, 53, 6)
     drain_x()
     drain_sums()
@@ -569,37 +584,23 @@
     keep[...] = jnp.broadcast_to(phit[:, 96:97], (128, 128))
 
     def split(ref, n):
-        c = jnp.concatenate([ref[pl.ds(pl.multiple_of(n * 48 + 16 * j, 16), 16), :] for j in range(3)], axis=1)
+        c = jnp.concatenate([ref[n * 96 + 16 * j : n * 96 + 16 * j + 16, :] for j in range(SLOT)], axis=1)
         hi = c.astype(BF16)
         lo = (c - hi.astype(F32)).astype(BF16)
         return jnp.concatenate([hi, lo, hi], axis=0)
 
     def put(n):
-        cols = pl.ds(pl.multiple_of(n * 384, 128), 384)
-        return pltpu.make_async_copy(buf.at[n % BUFS], out.at[:, :, cols], out_sem.at[n % BUFS])
-
-    def relaxed(n, _):
-        @pl.when(n >= BUFS)
-        def _():
-            put(n - BUFS).wait()
-
+        return pltpu.make_async_copy(buf.at[n], out.at[:, :, n * 768 : (n + 1) * 768], out_sem.at[n])
+
+    for n in range(8):
         poly = jnp.dot(lhs_f, split(coef_f, n), preferred_element_type=F32)
         power = jnp.dot(lhs_l, split(coef_l, n), preferred_element_type=F32)
-        for j in range(3):
-            cols = pl.ds(pl.multiple_of(n * 384 + j * 128, 128), 128)
+        for j in range(SLOT):
             part = slice(j * 128, (j + 1) * 128)
-            swept = val[:, :, cols].reshape(128, 128)
-            buf[n % BUFS, :, :, part] = (keep[...] * swept + poly[:, part] * jnp.exp2(power[:, part])).reshape(2, 64, 128)
+            swept = val[:, :, n * 768 + j * 128 : n * 768 + (j + 1) * 128].reshape(128, 128)
+            buf[n, :, :, part] = (keep[...] * swept + poly[:, part] * jnp.exp2(power[:, part])).reshape(2, 64, 128)
         put(n).start()
-        return 0
-
-    def two(n, _):
-        relaxed(2 * n, 0)
-        relaxed(2 * n + 1, 0)
-        return 0
-
-    lax.fori_loop(0, 8, two, 0)
-    for n in range(16 - BUFS, 16):
+    for n in range(8):
         put(n).wait()
     mac_copy.wait()
 
@@ -622,12 +623,13 @@
             pltpu.VMEM((3, 2, 64), F32),
             pltpu.VMEM((13, 2, 64), F32),
             pltpu.VMEM((2, 64), F32),
+            pltpu.VMEM((96, 6144), BF16),
             pltpu.VMEM((512, 128), BF16),
             pltpu.VMEM((2, 64, 6144), F32),
             pltpu.VMEM((2, 64, 6144), F32),
             pltpu.VMEM((2, 64, 6144), F32),
-            pltpu.VMEM((2, 64, 256), F32),
-            pltpu.VMEM((2, 3, 64, 256), F32),
+            pltpu.VMEM((2, 104, 128), F32),
+            pltpu.VMEM((2, 3, 104, 128), F32),
             pltpu.VMEM((2, 64, 384), F32),
             pltpu.VMEM((32, 256), F32),
             pltpu.VMEM((128, 128), F32),
@@ -636,8 +638,9 @@
             pltpu.VMEM((4 * SLOT_ROWS, 128), F32),
             pltpu.VMEM((3 * SLOT_ROWS, 128), F32),
             pltpu.VMEM((7 * 16, 128), F32),
-            pltpu.VMEM((10 * SLOT_ROWS, 128), F32),
-            pltpu.VMEM((10 * SLOT_ROWS, 128), F32),
+            pltpu.VMEM((10 * SLOT_ROWS + 8, 128), F32),
+            pltpu.VMEM((60 * 16, 128), F32),
+            pltpu.VMEM((60 * 16, 128), F32),
             pltpu.SemaphoreType.DMA((8,)),
             pltpu.SemaphoreType.DMA((4,)),
             pltpu.SemaphoreType.DMA((N_SEM,)),
@@ -660,8 +663,8 @@
             pltpu.VMEM((TILES * 16, 128), F32),
             pltpu.VMEM((TILES * 16, 128), F32),
             pltpu.VMEM((128, 128), F32),
-            pltpu.VMEM((BUFS, 2, 64, 384), F32),
-            pltpu.SemaphoreType.DMA((BUFS,)),
+            pltpu.VMEM((8, 2, 64, 768), F32),
+            pltpu.SemaphoreType.DMA((8,)),
             pltpu.SemaphoreType.DMA,
         ],
         compiler_params=pltpu.CompilerParams(vmem_limit_bytes=32 * 2**20),

time: 46.7 us -> 41.1 us (0.88)
  Pallas kernels: 46 us -> 40.3 us
    pallas_call x1, Pallas kernels: 41.1 us -> 38 us  [per_device(): pl.pallas_call(kernel, out_shape=(jax.ShapeDtypeStruct((2, 64, 6144), F32...]
    pallas_call x1, Pallas kernels: 4.88 us -> 2.38 us  [per_device(): pl.pallas_call(relax_kernel, out_shape=(jax.ShapeDtypeStruct((2, 64, 6144...]
where the time goes in v4:
time: 41.1 us; the launch traced here: 41 us
  Pallas kernels  40.3 us (98%)
  between operations  0.64 us (2%)
    pallas_call x1, Pallas kernels, per_device(): pl.pallas_call(kernel, out_shape=(jax.ShapeDtypeStruct((2, 64, 6144), F32...  38 us
    pallas_call x1, Pallas kernels, per_device(): pl.pallas_call(relax_kernel, out_shape=(jax.ShapeDtypeStruct((2, 64, 6144...  2.38 us

profile of v4, /device:TPU:1, one launch (start us, length us, event | category | flops | bytes accessed | tf_op | source)
XLA Modules:
  0.0 41.0 jit_solution(9563217188927949553)
XLA Ops:
  0.6 38.0 %shard_map.68 = (f32[2,64,6144]{2,1,0:T(8,128)S(1)}, f32[768,128]{1,0:T(8,128)S(1)}, f32[128,128]{1,0:T(8,128)S(1)}) custom-call(f32[2,64,6144]{2,1,0:T(8,128)} %dist.1, f32[2,32,64]{2,1,0:T(8,128)} %bitcast.1, f32[3,2,64]{2,1,0:T(2,128)} %vel_hbm.1, f32[13,2,64]{2,1,0:T(2,128)} %wgt_hbm.1, f32[2,64]{1,0:T(2,128)} %rel_hbm.1), custom_call_target="tpu_custom_call" | custom-call | tf_op jit(solution)/shard_map/pallas_call | solution.py:612
  38.6 2.4 %shard_map.69 = (f32[2,64,6144]{2,1,0:T(8,128)}, f32[13,6144]{1,0:T(8,128)}) custom-call(f32[2,64,6144]{2,1,0:T(8,128)S(1)} %get-tuple-element.5.val, f32[768,128]{1,0:T(8,128)S(1)} %get-tuple-element.6.moved, f32[128,128]{1,0:T(8,128)S(1)} %get-tuple-element.7.phit), custom_call_target="tpu_custom_call" | custom-call | tf_op jit(solution)/shard_map/pallas_call | solution.py:653

commit v5 on v4

--- a/solution.py
+++ b/solution.py
@@ -15,22 +15,21 @@
 NX, NY, NZ = 4, 4, 8
 TILES, SLOT = 48, 6
 SLOT_ROWS, OWNERS = 80, 5
-AWAY = (2, 1, 3, 0)
+AWAY = ((2, 1), (2, 0), (1, 1), (3, 1), (1, 0), (3, 0), (0, 1), (0, 0))
 
 XF, CR = 0, 6
-YR = CR + 4
-ZR = YR + 3
+ZR = CR + 7
 ZG = ZR + 7
 YG = ZG + 7
-CG = YG + 3
-HALO = CG + 5
+CG = YG + 7
+HALO = CG + 1
 N_SEM = HALO + 4
 
 
 def kernel(
     dist, fac_hbm, vel_hbm, wgt_hbm, rel_hbm, val, moved, phit,
     fac, vel, wgt, rel, picks, lhs, reach, scaled, spread_f, snd, rcv, inc, wmat, phi,
-    stage, part, got_c, got_y, got_z, full, tmp, again, ld_sem, small_sem, ssem, rsem,
+    stage, part, got, got_z, full, tmp, again, ld_sem, small_sem, ssem, rsem,
 ):
     gx = lax.axis_index("gx")
     vert = lax.axis_index("vert")
@@ -72,7 +71,8 @@
         greet((gx + t) % NX, vert)
     greet(gx, vert_of(y, z, 1 - core))
     for t in range(1, NY):
-        greet(gx, vert_of((y + t) % NY, z, core))
+        for core_ in (core, 1 - core):
+            greet(gx, vert_of((y + t) % NY, z, core_))
     for t in range(1, NZ):
         greet(gx, vert_of(y, (z + t) % NZ, core))
     has_left, has_right = gx > 0, gx < NX - 1
@@ -121,18 +121,13 @@
         lhs[n * 128 : (n + 1) * 128, :] = turned.astype(BF16)
         return turned
 
-    def spread(first, refs, unroll):
-        def some(n, _):
-            for k in range(unroll):
-                p = n * unroll + k
-                cols = pl.ds(pl.multiple_of(p * 384, 128), 384)
-                rows = lhs[first * 128 : (first + len(refs)) * 128, 0:96]
-                wide = jnp.dot(rows, picks[:, cols], preferred_element_type=F32)
-                for m, ref in enumerate(refs):
-                    ref[:, :, cols] = wide[m * 128 : (m + 1) * 128].reshape(2, 64, 384)
-            return 0
-
-        lax.fori_loop(0, 16 // unroll, some, 0)
+    def spread(first, refs):
+        for p in range(16):
+            cols = slice(p * 384, (p + 1) * 384)
+            rows = lhs[first * 128 : (first + len(refs)) * 128, 0:96]
+            wide = jnp.dot(rows, picks[:, cols], preferred_element_type=F32)
+            for m, ref in enumerate(refs):
+                ref[:, :, cols] = wide[m * 128 : (m + 1) * 128].reshape(2, 64, 384)
 
     phi[...] = exact(to_edge, 0, after)
 
@@ -194,7 +189,7 @@
     for d in range(2):
         leave(d)
         if d == 0:
-            pl.semaphore_wait(barrier, 14 + jnp.where(halo_source, 3, 0))
+            pl.semaphore_wait(barrier, 17 + jnp.where(halo_source, 3, 0))
         for t in (2, 1, 3):
             target = gx + t if d == 0 else gx - t
 
@@ -204,9 +199,9 @@
 
     for one_copy in small[1:]:
         one_copy.wait()
-    for n in range(4):
-        for ref in (stage, part):
-            ref[n * SLOT_ROWS + 72 : n * SLOT_ROWS + 80, :] = jnp.zeros((8, 128), F32)
+    for n in range(7):
+        stage[n * SLOT_ROWS + 72 : n * SLOT_ROWS + 80, :] = jnp.zeros((8, 128), F32)
+    part[72:80, :] = jnp.zeros((8, 128), F32)
     full[10 * SLOT_ROWS : 10 * SLOT_ROWS + 8, :] = jnp.zeros((8, 128), F32)
     wmat[...] = jnp.zeros_like(wmat)
     for k in range(13):
@@ -236,7 +231,7 @@
     exact(f, 1, f)
     exact(q, 2, q)
     exact(jnp.where(ahead, before, after), 3, f)
-    spread(1, [spread_f, scaled, reach], 2)
+    spread(1, [spread_f, scaled, reach])
 
     def sweep(r):
         rows = rows8(r)
@@ -336,41 +331,22 @@
 
     partner = vert_of(y, z, 1 - core)
 
-    def to_core(n):
-        return copy(stage.at[slot_rows(n), :], got_c.at[slot_rows(n), :], CR + n, CR + n, gx, partner)
-
-    def other_half(n, _):
-        moments((1 - core) * 4 + (y + AWAY[n]) % NY, stage, n * SLOT_ROWS)
-        to_core(n).start()
-        return 0
-
-    for n in range(4):
-        other_half(n, 0)
-
-    def to_y(n):
-        return copy(
-            part.at[slot_rows(n), :], got_y.at[slot_rows(n), :], YR + n, YR + n, gx, vert_of((y + AWAY[n]) % NY, z, core)
-        )
-
-    def own_half(n, _):
-        moments(core * 4 + (y + AWAY[n]) % NY, part, n * SLOT_ROWS)
-        to_core(n).wait_recv()
-        part[slot_rows(n), :] += got_c[slot_rows(n), :]
-
-        if n < 3:
-            to_y(n).start()
-
-    for n in range(4):
-        own_half(n, 0)
-    for n in range(3):
-        to_y(n).wait_recv()
-        part[slot_rows(3), :] += got_y[slot_rows(n), :]
+    def to_slot(n):
+        dy, dc = AWAY[n]
+        target = vert_of((y + dy) % NY, z, (core + dc) % 2)
+        return copy(stage.at[slot_rows(n), :], got.at[slot_rows(n), :], CR + n, CR + n, gx, target)
+
+    for n, (dy, dc) in enumerate(AWAY):
+        moments((core + dc) % 2 * 4 + (y + dy) % NY, stage if n < 7 else part, n % 7 * SLOT_ROWS)
+        if n < 7:
+            to_slot(n).start()
+    for n in (6, 4, 5, 2, 3, 1, 0):
+        to_slot(n).wait_recv()
+        part[...] += got[slot_rows(n), :]
 
     def drain_sums():
-        for n in range(4):
-            to_core(n).wait_send()
-        for n in range(3):
-            to_y(n).wait_send()
+        for n in range(7):
+            to_slot(n).wait_send()
 
     def tile_rows(n):
         return pl.ds(pl.multiple_of(n * 16, 16), 16)
@@ -381,7 +357,7 @@
     def to_z(n):
         peer = (z + n + 1) % NZ
         return copy(
-            part.at[pl.ds(pl.multiple_of(3 * SLOT_ROWS + peer * 16, 16), 16), :], got_z.at[tile_rows(n), :],
+            part.at[pl.ds(pl.multiple_of(peer * 16, 16), 16), :], got_z.at[tile_rows(n), :],
             ZR + n, ZR + n, gx, vert_of(y, peer, core),
         )
 
@@ -403,7 +379,7 @@
 
     @pl.when(z < OWNERS)
     def _():
-        total = part[pl.ds(pl.multiple_of(3 * SLOT_ROWS + z * 16, 16), 16), :]
+        total = part[pl.ds(pl.multiple_of(z * 16, 16), 16), :]
         for n in range(7):
             copy(got_z.at[tile_rows(n), :], got_z.at[tile_rows(n), :], ZR + n, ZR + n, gx, vert).wait_recv()
             total += got_z[tile_rows(n), :]
@@ -421,10 +397,14 @@
     def slot_of(n):
         return pl.ds(pl.multiple_of((1 + n) * SLOT_ROWS, SLOT_ROWS), SLOT_ROWS)
 
-    def gather_y(n, slot):
-        return copy(
-            full.at[slot_of(slot), :], full.at[slot_of(slot), :], YG + n, YG + n, gx, vert_of((y + n + 1) % NY, z, core)
-        )
+    def gather(n, slot):
+        dy, dc = AWAY[n]
+        target = vert_of((y + dy) % NY, z, (core + dc) % 2)
+        return copy(full.at[slot_of(slot), :], full.at[slot_of(slot), :], YG + n, YG + n, gx, target)
+
+    def slot_from(n):
+        dy, dc = AWAY[n]
+        return (core + dc) % 2 * 4 + (y + NY - dy) % NY
 
     halo_slot = jnp.where(core == 1, -1, 8)
 
@@ -434,27 +414,21 @@
             jnp.where(core == 1, gx + 1, gx - 1), vert_of((y + n) % NY, z, core),
         )
 
-    def gather_core(n, slot):
-        return copy(full.at[slot_of(slot), :], full.at[slot_of(slot), :], CG + n, CG + n, gx, partner)
+    def relay_halo(slot):
+        return copy(full.at[slot_of(slot), :], full.at[slot_of(slot), :], CG, CG, gx, partner)
 
     @pl.when(halo_source)
     def _():
         for n in (2, 1, 3, 0):
             send_halo(n).start()
 
-    for n in (1, 0, 2):
-        gather_y(n, mine).start()
-
-    gather_core(3, mine).start()
-    for n in (0, 2, 1):
-        slot = core * 4 + (y + NY - n - 1) % NY
-        gather_y(n, slot).wait_recv()
-        gather_core(n, slot).start()
+    for n in range(7):
+        gather(n, mine).start()
 
     @pl.when(halo_here)
     def _():
         copy(full.at[slot_of(halo_slot), :], full.at[slot_of(halo_slot), :], HALO, HALO, gx, vert).wait_recv()
-        gather_core(4, halo_slot).start()
+        relay_halo(halo_slot).start()
 
     nothing = jnp.zeros((SLOT_ROWS, 128), F32)
 
@@ -466,29 +440,26 @@
     def _():
         full[slot_of(8), :] = nothing
 
-    for n in range(4):
-        gather_core(n, (1 - core) * 4 + (y + NY - n - 1) % NY).wait_recv()
+    for n in range(7):
+        gather(n, slot_from(n)).wait_recv()
 
     other_halo = jnp.where(core == 1, 8, -1)
 
     @pl.when(jnp.where(core == 1, has_right, has_left))
     def _():
-        gather_core(4, other_halo).wait_recv()
-
-    for n in range(3):
-        gather_y(n, mine).wait_send()
+        relay_halo(other_halo).wait_recv()
+
+    for n in range(7):
+        gather(n, mine).wait_send()
 
     @pl.when(halo_source)
     def _():
         for n in range(4):
             send_halo(n).wait_send()
 
-    for n in range(4):
-        gather_core(n, core * 4 + (y + NY - n - 1) % NY).wait_send()
-
     @pl.when(halo_here)
     def _():
-        gather_core(4, halo_slot).wait_send()
+        relay_halo(halo_slot).wait_send()
 
     @pl.when(z < OWNERS)
     def _():
@@ -633,10 +604,9 @@
             pltpu.VMEM((2, 64, 384), F32),
             pltpu.VMEM((32, 256), F32),
             pltpu.VMEM((128, 128), F32),
-            pltpu.VMEM((4 * SLOT_ROWS, 128), F32),
-            pltpu.VMEM((4 * SLOT_ROWS, 128), F32),
-            pltpu.VMEM((4 * SLOT_ROWS, 128), F32),
-            pltpu.VMEM((3 * SLOT_ROWS, 128), F32),
+            pltpu.VMEM((7 * SLOT_ROWS, 128), F32),
+            pltpu.VMEM((SLOT_ROWS, 128), F32),
+            pltpu.VMEM((7 * SLOT_ROWS, 128), F32),
             pltpu.VMEM((7 * 16, 128), F32),
             pltpu.VMEM((10 * SLOT_ROWS + 8, 128), F32),
             pltpu.VMEM((60 * 16, 128), F32),

time: 41.1 us -> 40.7 us (level)
    pallas_call x1, Pallas kernels: 38 us -> 37.5 us  [per_device(): pl.pallas_call(kernel, out_shape=(jax.ShapeDtypeStruct((2, 64, 6144), F32...]
where the time goes in v5:
time: 40.7 us; the launch traced here: 40.6 us
  Pallas kernels  39.9 us (98%)
  between operations  0.64 us (2%)
    pallas_call x1, Pallas kernels, per_device(): pl.pallas_call(kernel, out_shape=(jax.ShapeDtypeStruct((2, 64, 6144), F32...  37.5 us
    pallas_call x1, Pallas kernels, per_device(): pl.pallas_call(relax_kernel, out_shape=(jax.ShapeDtypeStruct((2, 64, 6144...  2.38 us

profile of v5, /device:TPU:1, one launch (start us, length us, event | category | flops | bytes accessed | tf_op | source)
XLA Modules:
  0.0 40.6 jit_solution(7119639740145571798)
XLA Ops:
  0.6 37.5 %shard_map.68 = (f32[2,64,6144]{2,1,0:T(8,128)S(1)}, f32[768,128]{1,0:T(8,128)S(1)}, f32[128,128]{1,0:T(8,128)S(1)}) custom-call(f32[2,64,6144]{2,1,0:T(8,128)} %dist.1, f32[2,32,64]{2,1,0:T(8,128)} %bitcast.1, f32[3,2,64]{2,1,0:T(2,128)} %vel_hbm.1, f32[13,2,64]{2,1,0:T(2,128)} %wgt_hbm.1, f32[2,64]{1,0:T(2,128)} %rel_hbm.1), custom_call_target="tpu_custom_call" | custom-call | tf_op jit(solution)/shard_map/pallas_call | solution.py:583
  38.2 2.4 %shard_map.69 = (f32[2,64,6144]{2,1,0:T(8,128)}, f32[13,6144]{1,0:T(8,128)}) custom-call(f32[2,64,6144]{2,1,0:T(8,128)S(1)} %get-tuple-element.5.val, f32[768,128]{1,0:T(8,128)S(1)} %get-tuple-element.6.moved, f32[128,128]{1,0:T(8,128)S(1)} %get-tuple-element.7.phit), custom_call_target="tpu_custom_call" | custom-call | tf_op jit(solution)/shard_map/pallas_call | solution.py:623

commit v6 on v5

--- a/solution.py
+++ b/solution.py
@@ -59,7 +59,7 @@
     ]
     for one_copy in small:
         one_copy.start()
-    for r in range(8):
+    for r in (0, 4, 1, 5, 2, 6, 3, 7):
         load(r).start()
 
     barrier = pltpu.get_barrier_semaphore()
@@ -143,15 +143,19 @@
     def half_row(pair):
         return 72 + 8 * pair
 
-    def leave(d):
+    def leave():
         total = None
         for p in range(16):
             if p % 4 == 0:
-                load(d * 4 + p // 4).wait()
+                load(p // 4).wait()
+                load(4 + p // 4).wait()
             cols = slice(p * 384, (p + 1) * 384)
-            weight = jnp.dot(lhs[d * 64 : d * 64 + 64, 0:96], picks[:, cols], preferred_element_type=F32)
-            term = weight * val[d, :, cols]
+            weight = jnp.dot(lhs[0:128, 0:64], picks[0:64, cols], preferred_element_type=F32)
+            term = weight * val[:, :, cols].reshape(128, 384)
             total = term if total is None else total + term
+        return total
+
+    def pack(d, total):
         halves = []
         for r in range(8):
             a, b, c = [total[8 * r : 8 * r + 8, j * 128 : (j + 1) * 128] for j in range(3)]
@@ -186,8 +190,9 @@
             def _():
                 edge(1, t, (gx - t) % NX).wait_send()
 
+    leaving = leave()
     for d in range(2):
-        leave(d)
+        pack(d, leaving[d * 64 : d * 64 + 64])
         if d == 0:
             pl.semaphore_wait(barrier, 17 + jnp.where(halo_source, 3, 0))
         for t in (2, 1, 3):

time: 40.7 us -> 39.9 us (0.980)
  Pallas kernels: 39.9 us -> 39.1 us
    pallas_call x1, Pallas kernels: 37.5 us -> 36.8 us  [per_device(): pl.pallas_call(kernel, out_shape=(jax.ShapeDtypeStruct((2, 64, 6144), F32...]
where the time goes in v6:
time: 39.9 us; the launch traced here: 39.8 us
  Pallas kernels  39.1 us (98%)
  between operations  0.64 us (2%)
    pallas_call x1, Pallas kernels, per_device(): pl.pallas_call(kernel, out_shape=(jax.ShapeDtypeStruct((2, 64, 6144), F32...  36.8 us
    pallas_call x1, Pallas kernels, per_device(): pl.pallas_call(relax_kernel, out_shape=(jax.ShapeDtypeStruct((2, 64, 6144...  2.38 us

profile of v6, /device:TPU:1, one launch (start us, length us, event | category | flops | bytes accessed | tf_op | source)
XLA Modules:
  0.0 39.8 jit_solution(6250794682028920234)
XLA Ops:
  0.6 36.8 %shard_map.68 = (f32[2,64,6144]{2,1,0:T(8,128)S(1)}, f32[768,128]{1,0:T(8,128)S(1)}, f32[128,128]{1,0:T(8,128)S(1)}) custom-call(f32[2,64,6144]{2,1,0:T(8,128)} %dist.1, f32[2,32,64]{2,1,0:T(8,128)} %bitcast.1, f32[3,2,64]{2,1,0:T(2,128)} %vel_hbm.1, f32[13,2,64]{2,1,0:T(2,128)} %wgt_hbm.1, f32[2,64]{1,0:T(2,128)} %rel_hbm.1), custom_call_target="tpu_custom_call" | custom-call | tf_op jit(solution)/shard_map/pallas_call | solution.py:588
  37.4 2.4 %shard_map.69 = (f32[2,64,6144]{2,1,0:T(8,128)}, f32[13,6144]{1,0:T(8,128)}) custom-call(f32[2,64,6144]{2,1,0:T(8,128)S(1)} %get-tuple-element.5.val, f32[768,128]{1,0:T(8,128)S(1)} %get-tuple-element.6.moved, f32[128,128]{1,0:T(8,128)S(1)} %get-tuple-element.7.phit), custom_call_target="tpu_custom_call" | custom-call | tf_op jit(solution)/shard_map/pallas_call | solution.py:628

commit v7 on v6

--- a/solution.py
+++ b/solution.py
@@ -316,7 +316,7 @@
     entering(0)
     entering(1)
 
-    weights = wmat[...].astype(BF16)
+    weights = wmat[0:32, :].astype(BF16)
 
     def moments(slot, dst, dst_row):
         for half in range(2):
@@ -347,7 +347,7 @@
             to_slot(n).start()
     for n in (6, 4, 5, 2, 3, 1, 0):
         to_slot(n).wait_recv()
-        part[...] += got[slot_rows(n), :]
+        part[0:SLOT_ROWS, :] += got[slot_rows(n), :]
 
     def drain_sums():
         for n in range(7):
@@ -607,10 +607,10 @@
             pltpu.VMEM((2, 104, 128), F32),
             pltpu.VMEM((2, 3, 104, 128), F32),
             pltpu.VMEM((2, 64, 384), F32),
-            pltpu.VMEM((32, 256), F32),
+            pltpu.VMEM((40, 256), F32),
             pltpu.VMEM((128, 128), F32),
-            pltpu.VMEM((7 * SLOT_ROWS, 128), F32),
-            pltpu.VMEM((SLOT_ROWS, 128), F32),
+            pltpu.VMEM((7 * SLOT_ROWS + 8, 128), F32),
+            pltpu.VMEM((SLOT_ROWS + 8, 128), F32),
             pltpu.VMEM((7 * SLOT_ROWS, 128), F32),
             pltpu.VMEM((7 * 16, 128), F32),
             pltpu.VMEM((10 * SLOT_ROWS + 8, 128), F32),

time: 39.9 us -> 39.9 us (level)
  no operation moved by 1% of the time
where the time goes in v7:
time: 39.9 us; the launch traced here: 39.8 us
  Pallas kernels  39.1 us (98%)
  between operations  0.64 us (2%)
    pallas_call x1, Pallas kernels, per_device(): pl.pallas_call(kernel, out_shape=(jax.ShapeDtypeStruct((2, 64, 6144), F32...  36.8 us
    pallas_call x1, Pallas kernels, per_device(): pl.pallas_call(relax_kernel, out_shape=(jax.ShapeDtypeStruct((2, 64, 6144...  2.38 us

profile of v7, /device:TPU:1, one launch (start us, length us, event | category | flops | bytes accessed | tf_op | source)
XLA Modules:
  0.0 39.8 jit_solution(645406891919550516)
XLA Ops:
  0.6 36.8 %shard_map.68 = (f32[2,64,6144]{2,1,0:T(8,128)S(1)}, f32[768,128]{1,0:T(8,128)S(1)}, f32[128,128]{1,0:T(8,128)S(1)}) custom-call(f32[2,64,6144]{2,1,0:T(8,128)} %dist.1, f32[2,32,64]{2,1,0:T(8,128)} %bitcast.1, f32[3,2,64]{2,1,0:T(2,128)} %vel_hbm.1, f32[13,2,64]{2,1,0:T(2,128)} %wgt_hbm.1, f32[2,64]{1,0:T(2,128)} %rel_hbm.1), custom_call_target="tpu_custom_call" | custom-call | tf_op jit(solution)/shard_map/pallas_call | solution.py:588
  37.4 2.4 %shard_map.69 = (f32[2,64,6144]{2,1,0:T(8,128)}, f32[13,6144]{1,0:T(8,128)}) custom-call(f32[2,64,6144]{2,1,0:T(8,128)S(1)} %get-tuple-element.5.val, f32[768,128]{1,0:T(8,128)S(1)} %get-tuple-element.6.moved, f32[128,128]{1,0:T(8,128)S(1)} %get-tuple-element.7.phit), custom_call_target="tpu_custom_call" | custom-call | tf_op jit(solution)/shard_map/pallas_call | solution.py:628
